TPU v7x, 512 devices: a whole 4x4x16 slice. The times are simulated.
512 devices in a mesh: blk: 32 (over y_lo, z), gy: 4 (over x), rep: 4 (over y_hi, core).
Axes of the slice: x: 4, y: 4 (y_hi: 2, y_lo: 2; y = y_hi * 2 + y_lo), z: 16, core: 2. Of those that a mesh axis runs over, the one named last changes fastest.
Arguments:
- grain_id: int32 [128, 32, 512], P('blk', 'gy', 'rep'), may hold values from 0 to 255
- init_masks: int32 [2, 128, 32, 512], P(None, 'blk', 'gy', 'rep'), may hold values from 0 to 1, as said below
- target_masks: int32 [2, 128, 32, 512], P(None, 'blk', 'gy', 'rep'), may hold values from 0 to 1, as said below
- emb_table: bfloat16 [256, 8], replicated, may hold values from -6 to 6
- w_in: float32 [64, 10], P('rep'), may hold values from -2 to 2
- b_in: float32 [64], P('rep'), may hold values from -3 to 3
- w_mid: float32 [64, 64], P('rep'), may hold values from -0.75 to 0.75
- b_mid: float32 [64], P('rep'), may hold values from -3 to 3
- w_out: float32 [6, 64], P(None, 'rep'), may hold values from -0.75 to 0.75
- b_out: float32 [6], replicated, may hold values from -4 to 4
Outputs:
- final_state: float32 [2, 128, 32, 512], P(None, 'blk', 'gy', 'rep')
- loss: float32 [], replicated
- grad_w_in: float32 [64, 10], P('rep')
- grad_b_in: float32 [64], P('rep')
- grad_w_mid: float32 [64, 64], P('rep')
- grad_b_mid: float32 [64], P('rep')
- grad_w_out: float32 [6, 64], P(None, 'rep')
- grad_b_out: float32 [6], replicated
- start_sensitivity: float32 [2, 128, 32, 512], P(None, 'blk', 'gy', 'rep')
Inputs may be any that keep to these rules, and one draw needn't show every extreme that they name: `init_masks`: 0 or 1 in every cell. `target_masks`: 0 or 1 in every cell.
All inputs are finite; a program needn't handle non-finite values.
Results may differ from a plain program's by a relative error of at most 0.0054.
The roundings to bfloat16 on the way count: a program that leaves them out, or rounds other values in their place, can miss the bound.
Values may be sent and summed in bfloat16 or wider, within the bound.
A program may use at most 64 MiB of HBM per device.

v0:
```python
import jax
import jax.numpy as jnp
from jax import lax
from jax.sharding import PartitionSpec as P

STEPS = 4
RATE_MAX = 0.15


def extended(block, sides, width):
    for axis, dim in sides:
        count = lax.axis_size(axis)
        forward = [(i, i + 1) for i in range(count - 1)]
        forward.append((count - 1, 0))
        backward = [(target, source) for source, target in forward]
        low = lax.ppermute(
            lax.slice_in_dim(block, block.shape[dim] - width, None, axis=dim), axis, forward
        )
        high = lax.ppermute(lax.slice_in_dim(block, 0, width, axis=dim), axis, backward)
        block = jnp.concatenate([low, block, high], axis=dim)
    return block


def beside(padded, axis_pos, offset):
    index_list = [slice(None), slice(1, -1), slice(1, -1), slice(1, -1)]
    index_list[axis_pos] = slice(1 + offset, padded.shape[axis_pos] - 1 + offset)
    return padded[tuple(index_list)]


def interior(padded):
    return padded[:, 1:-1, 1:-1, 1:-1]


def diffuse(field_pad, rate_pad):
    centre = interior(field_pad)
    summed = centre
    rate_centre = interior(rate_pad)
    for direction in range(3):
        axis_pos = 3 - direction
        rate_here = rate_centre[direction::3]
        for offset in (1, -1):
            rate_next = beside(rate_pad, axis_pos, offset)[direction::3]
            summed = summed + 0.5 * (rate_here + rate_next) * (
                beside(field_pad, axis_pos, offset) - centre
            )
    return summed


def rate_cotangent(state_pad, adjoint_pad):
    centre_state = interior(state_pad)
    centre_adjoint = interior(adjoint_pad)
    pieces_list = []
    for direction in range(3):
        axis_pos = 3 - direction
        summed = jnp.zeros_like(centre_state)
        for offset in (1, -1):
            summed = summed + (beside(state_pad, axis_pos, offset) - centre_state) * (
                beside(adjoint_pad, axis_pos, offset) - centre_adjoint
            )
        pieces_list.append(-0.5 * summed)
    stacked = jnp.stack(pieces_list, axis=1)
    return stacked.reshape((6,) + stacked.shape[2:])


def embed_lookup(emb_table, grain_flat):
    table_rows = emb_table.shape[0]
    one_hot = (grain_flat[None, :] == lax.broadcasted_iota(jnp.int32, (table_rows, 1), 0)).astype(
        jnp.bfloat16
    )
    looked = jnp.dot(emb_table.T, one_hot, preferred_element_type=jnp.float32)
    return looked.astype(jnp.bfloat16)


def forward_layers(params, features):
    w_in, b_in, w_mid, b_mid, w_out, b_out = params
    act_one = jnp.tanh(
        jnp.dot(w_in, features, preferred_element_type=jnp.float32)
        + b_in.astype(jnp.float32)[:, None]
    )
    hid_one = act_one.astype(jnp.bfloat16)
    act_two = jnp.tanh(
        jnp.dot(w_mid, hid_one, preferred_element_type=jnp.float32)
        + b_mid.astype(jnp.float32)[:, None]
    )
    hid_two = act_two.astype(jnp.bfloat16)
    logits = (
        jnp.dot(w_out, hid_two, preferred_element_type=jnp.float32)
        + b_out.astype(jnp.float32)[:, None]
    )
    return (RATE_MAX * jax.nn.sigmoid(logits), act_one, hid_one, act_two, hid_two)


def backward_layers(params, features, rate_grad, forward_values):
    w_in, b_in, w_mid, b_mid, w_out, b_out = params
    rate_values, act_one, hid_one, act_two, hid_two = forward_values
    out_grad = (rate_grad * rate_values * (1.0 - rate_values / RATE_MAX)).astype(jnp.bfloat16)
    two_grad = (
        jnp.dot(w_out.T, out_grad, preferred_element_type=jnp.float32) * (1.0 - act_two * act_two)
    ).astype(jnp.bfloat16)
    one_grad = (
        jnp.dot(w_mid.T, two_grad, preferred_element_type=jnp.float32) * (1.0 - act_one * act_one)
    ).astype(jnp.bfloat16)
    grad_terms = (
        jnp.dot(one_grad, features.T, preferred_element_type=jnp.float32),
        jnp.sum(one_grad, axis=1, dtype=jnp.float32),
        jnp.dot(two_grad, hid_one.T, preferred_element_type=jnp.float32),
        jnp.sum(two_grad, axis=1, dtype=jnp.float32),
        jnp.dot(out_grad, hid_two.T, preferred_element_type=jnp.float32),
        jnp.sum(out_grad, axis=1, dtype=jnp.float32),
    )
    state_grad = jnp.dot(w_in[:, -2:].T, one_grad, preferred_element_type=jnp.float32)
    return (grad_terms, state_grad)


def per_device(
    grain_id, init_masks, target_masks, emb_table, w_in, b_in, w_mid, b_mid, w_out, b_out
):
    w_in_b, b_in_b, w_mid_b, b_mid_b, w_out_b = (
        lax.all_gather(w_in.astype(jnp.bfloat16), "rep", axis=0, tiled=True),
        lax.all_gather(b_in.astype(jnp.bfloat16), "rep", axis=0, tiled=True),
        lax.all_gather(w_mid.astype(jnp.bfloat16), "rep", axis=0, tiled=True),
        lax.all_gather(b_mid.astype(jnp.bfloat16), "rep", axis=0, tiled=True),
        lax.all_gather(w_out.astype(jnp.bfloat16), "rep", axis=1, tiled=True),
    )
    params = (w_in_b, b_in_b, w_mid_b, b_mid_b, w_out_b, b_out.astype(jnp.bfloat16))
    depth_cells, row_cells, col_cells = grain_id.shape
    cell_count = depth_cells * row_cells * col_cells
    embedding = embed_lookup(emb_table, grain_id.reshape(cell_count))
    state_now = init_masks.astype(jnp.float32)
    history = []
    for step_index in range(STEPS):
        features = jnp.concatenate(
            [embedding, state_now.reshape(2, cell_count).astype(jnp.bfloat16)], axis=0
        )
        rate_values = forward_layers(params, features)[0].reshape(
            6, depth_cells, row_cells, col_cells
        )
        joined = extended(
            jnp.concatenate([state_now, rate_values], axis=0),
            (("blk", 1), ("gy", 2), ("rep", 3)),
            1,
        )
        state_pad = joined[:2]
        rate_pad = joined[2:]
        history.append((state_pad, rate_pad))
        state_now = diffuse(state_pad, rate_pad)
    misfit = state_now - target_masks.astype(jnp.float32)
    total_cells = float(
        cell_count * lax.axis_size("blk") * lax.axis_size("gy") * lax.axis_size("rep")
    )
    loss_part = jnp.sum(misfit * misfit) / (4.0 * total_cells)
    adjoint = misfit / (2.0 * total_cells)
    grad_sums = None
    for step_index in reversed(range(STEPS)):
        state_pad, rate_pad = history[step_index]
        adjoint_pad = extended(adjoint, (("blk", 1), ("gy", 2), ("rep", 3)), 1)
        rate_grad = rate_cotangent(state_pad, adjoint_pad).reshape(6, cell_count)
        features = jnp.concatenate(
            [embedding, interior(state_pad).reshape(2, cell_count).astype(jnp.bfloat16)], axis=0
        )
        forward_values = forward_layers(params, features)
        step_terms, state_grad = backward_layers(params, features, rate_grad, forward_values)
        if grad_sums is None:
            grad_sums = step_terms
        else:
            grad_sums = tuple(
                (earlier + later_term for earlier, later_term in zip(grad_sums, step_terms))
            )
        adjoint = diffuse(adjoint_pad, rate_pad) + state_grad.reshape(
            2, depth_cells, row_cells, col_cells
        )
    start_sensitivity = adjoint * (2.0 * total_cells)
    sum_w_in, sum_b_in, sum_w_mid, sum_b_mid, sum_w_out, sum_b_out = grad_sums
    summed = lax.psum(
        (sum_w_in, sum_b_in, sum_w_mid, sum_b_mid, sum_w_out, sum_b_out, loss_part),
        ("blk", "gy", "rep"),
    )
    position = lax.axis_index("rep")
    share_width = w_in.shape[0]
    grad_w_in = lax.dynamic_slice_in_dim(summed[0], position * share_width, share_width, 0)
    grad_b_in = lax.dynamic_slice_in_dim(summed[1], position * share_width, share_width, 0)
    grad_w_mid = lax.dynamic_slice_in_dim(summed[2], position * share_width, share_width, 0)
    grad_b_mid = lax.dynamic_slice_in_dim(summed[3], position * share_width, share_width, 0)
    grad_w_out = lax.dynamic_slice_in_dim(summed[4], position * share_width, share_width, 1)
    grad_b_out = summed[5]
    loss_total = summed[6]
    return (
        state_now,
        loss_total,
        grad_w_in,
        grad_b_in,
        grad_w_mid,
        grad_b_mid,
        grad_w_out,
        grad_b_out,
        start_sensitivity,
    )


def solution(mesh):
    in_specs = (
        P("blk", "gy", "rep"),
        P(None, "blk", "gy", "rep"),
        P(None, "blk", "gy", "rep"),
        P(),
        P("rep", None),
        P("rep"),
        P("rep", None),
        P("rep"),
        P(None, "rep"),
        P(),
    )
    out_specs = (
        P(None, "blk", "gy", "rep"),
        P(),
        P("rep", None),
        P("rep"),
        P("rep", None),
        P("rep"),
        P(None, "rep"),
        P(),
        P(None, "blk", "gy", "rep"),
    )
    return jax.shard_map(
        per_device, mesh=mesh, in_specs=in_specs, out_specs=out_specs, check_vma=False
    )
```

profile of v0, /device:TPU:1, one launch (start us, length us, event | category | flops | bytes accessed | tf_op | source)
XLA Modules:
  0.0 452.5 jit_solution(13899464881031292997)
XLA Ops:
  5.0 13.4 %all-reduce.3 = (bf16[64]{0:T(256)(128)(2,1)S(1)}, bf16[64]{0:T(256)(128)(2,1)S(1)}) all-reduce(bf16[64]{0:T(256)(128)(2,1)S(1)} %dynamic-update-slice.1, bf16[64]{0:T(256)(128)(2,1)S(1)} %dynamic-update-slice), channel_id=1, replica_groups=mesh['blk'=32,'gy'=4,'rep'=4] {'rep'}, use_global_device_ids=true, to_apply=%add.1 | all-reduce | flops 128 | bytes 512
  20.5 7.2 %all-gather = bf16[4,16,6]{1,2,0:T(8,128)(2,1)S(1)} all-gather(bf16[1,16,6]{1,2,0:T(8,128)(2,1)S(1)} %convert_bitcast_fusion.4), channel_id=1, replica_groups=mesh['blk'=32,'gy'=4,'rep'=4] {'rep'}, dimensions={0}, use_global_device_ids=true | all-gather | bytes 960 | tf_op jit(solution)/shard_map/all_gather | solution.py:123
  27.8 6.7 %all_gather.17 = bf16[64,64]{1,0:T(8,128)(2,1)S(1)} all-gather(bf16[16,64]{1,0:T(8,128)(2,1)S(1)} %convert_element_type.210), channel_id=1, replica_groups=mesh['blk'=32,'gy'=4,'rep'=4] {'rep'}, dimensions={0}, use_global_device_ids=true | all-gather | bytes 10240 | tf_op jit(solution)/shard_map/all_gather | solution.py:121
  34.5 6.7 %all_gather.15 = bf16[64,10]{1,0:T(8,128)(2,1)S(1)} all-gather(bf16[16,10]{1,0:T(8,128)(2,1)S(1)} %convert_element_type.206), channel_id=1, replica_groups=mesh['blk'=32,'gy'=4,'rep'=4] {'rep'}, dimensions={0}, use_global_device_ids=true | all-gather | bytes 1600 | tf_op jit(solution)/shard_map/all_gather | solution.py:119
  44.3 8.7 %collective-permute-start.1 = (f32[8,1,8,128]{3,2,1,0:T(8,128)S(1)}, f32[8,1,8,128]{3,2,1,0:T(8,128)S(1)}, u32[]{:S(2)}, u32[]{:S(2)}) collective-permute-start(f32[8,1,8,128]{3,2,1,0:T(8,128)S(1)} %get-tuple-element.100), channel_id=1, source_target_pairs={{16,0},{32,16},{48,32},{64,48},{80,64},{96,80},{112,96},{128,112},... | collective-permute-start | bytes 98312 | tf_op jit(solution)/shard_map/ppermute | solution.py:19
  54.9 4.8 %collective-permute-done = f32[8,1,8,128]{3,2,1,0:T(8,128)S(1)} collective-permute-done((f32[8,1,8,128]{3,2,1,0:T(8,128)S(1)}, f32[8,1,8,128]{3,2,1,0:T(8,128)S(1)}, u32[]{:S(2)}, u32[]{:S(2)}) %collective-permute-start) | collective-permute-done | bytes 32800 | tf_op jit(solution)/shard_map/ppermute | solution.py:16
  59.8 4.4 collective-permute-start.3
  66.2 3.7 collective-permute-done.2
  70.2 5.0 %collective-permute-start.4 = (f32[8,6,10,1]{3,2,1,0:T(8,128)S(1)}, f32[8,6,10,1]{3,2,1,0:T(8,128)S(1)}, u32[]{:S(2)}, u32[]{:S(2)}) collective-permute-start(f32[8,6,10,1]{3,2,1,0:T(8,128)S(1)} %get-tuple-element.64), channel_id=1, source_target_pairs={{1,0},{2,1},{3,2},{0,3},{5,4},{6,5},{7,6},{4,7},{9,8},{10,9},{11,1... | collective-permute-start | bytes 5768 | tf_op jit(solution)/shard_map/ppermute | solution.py:19
  75.2 3.3 collective-permute-start.5
  78.6 4.9 %collective-permute-done.4 = f32[8,6,10,1]{3,2,1,0:T(8,128)S(1)} collective-permute-done((f32[8,6,10,1]{3,2,1,0:T(8,128)S(1)}, f32[8,6,10,1]{3,2,1,0:T(8,128)S(1)}, u32[]{:S(2)}, u32[]{:S(2)}) %collective-permute-start.4) | collective-permute-done | bytes 1952 | tf_op jit(solution)/shard_map/ppermute | solution.py:19
  89.2 3.4 collective-permute-start.6
  92.6 3.4 collective-permute-done.6
  97.9 3.4 collective-permute-start.8
  104.0 6.9 %collective-permute-start.10 = (f32[8,6,10,1]{3,2,1,0:T(8,128)S(1)}, f32[8,6,10,1]{3,2,1,0:T(8,128)S(1)}, u32[]{:S(2)}, u32[]{:S(2)}) collective-permute-start(f32[8,6,10,1]{3,2,1,0:T(8,128)S(1)} %get-tuple-element.62), channel_id=1, source_target_pairs={{1,0},{2,1},{3,2},{0,3},{5,4},{6,5},{7,6},{4,7},{9,8},{10,9},{11,1... | collective-permute-start | bytes 5768 | tf_op jit(solution)/shard_map/ppermute | solution.py:19
  110.9 3.5 collective-permute-start.11
  114.4 5.1 %collective-permute-done.10 = f32[8,6,10,1]{3,2,1,0:T(8,128)S(1)} collective-permute-done((f32[8,6,10,1]{3,2,1,0:T(8,128)S(1)}, f32[8,6,10,1]{3,2,1,0:T(8,128)S(1)}, u32[]{:S(2)}, u32[]{:S(2)}) %collective-permute-start.10) | collective-permute-done | bytes 1952 | tf_op jit(solution)/shard_map/ppermute | solution.py:19
  124.9 3.4 collective-permute-start.12
  128.2 3.4 collective-permute-done.12
  133.6 3.4 collective-permute-start.14
  139.6 7.1 %collective-permute-start.16 = (f32[8,6,10,1]{3,2,1,0:T(8,128)S(1)}, f32[8,6,10,1]{3,2,1,0:T(8,128)S(1)}, u32[]{:S(2)}, u32[]{:S(2)}) collective-permute-start(f32[8,6,10,1]{3,2,1,0:T(8,128)S(1)} %get-tuple-element.60), channel_id=1, source_target_pairs={{1,0},{2,1},{3,2},{0,3},{5,4},{6,5},{7,6},{4,7},{9,8},{10,9},{11,1... | collective-permute-start | bytes 5768 | tf_op jit(solution)/shard_map/ppermute | solution.py:19
  146.7 3.3 collective-permute-start.17
  150.1 4.9 %collective-permute-done.16 = f32[8,6,10,1]{3,2,1,0:T(8,128)S(1)} collective-permute-done((f32[8,6,10,1]{3,2,1,0:T(8,128)S(1)}, f32[8,6,10,1]{3,2,1,0:T(8,128)S(1)}, u32[]{:S(2)}, u32[]{:S(2)}) %collective-permute-start.16) | collective-permute-done | bytes 1952 | tf_op jit(solution)/shard_map/ppermute | solution.py:19
  160.4 3.4 collective-permute-start.18
  163.8 3.4 collective-permute-done.18
  169.2 3.4 collective-permute-start.20
  175.2 7.1 %collective-permute-start.22 = (f32[8,6,10,1]{3,2,1,0:T(8,128)S(1)}, f32[8,6,10,1]{3,2,1,0:T(8,128)S(1)}, u32[]{:S(2)}, u32[]{:S(2)}) collective-permute-start(f32[8,6,10,1]{3,2,1,0:T(8,128)S(1)} %get-tuple-element.58), channel_id=1, source_target_pairs={{1,0},{2,1},{3,2},{0,3},{5,4},{6,5},{7,6},{4,7},{9,8},{10,9},{11,1... | collective-permute-start | bytes 5768 | tf_op jit(solution)/shard_map/ppermute | solution.py:19
  182.3 3.5 collective-permute-start.23
  185.9 5.1 %collective-permute-done.22 = f32[8,6,10,1]{3,2,1,0:T(8,128)S(1)} collective-permute-done((f32[8,6,10,1]{3,2,1,0:T(8,128)S(1)}, f32[8,6,10,1]{3,2,1,0:T(8,128)S(1)}, u32[]{:S(2)}, u32[]{:S(2)}) %collective-permute-start.22) | collective-permute-done | bytes 1952 | tf_op jit(solution)/shard_map/ppermute | solution.py:19
  195.6 5.5 %collective-permute-start.25 = (f32[2,1,8,128]{3,2,1,0:T(8,128)}, f32[2,1,8,128]{3,2,1,0:T(8,128)}, u32[]{:S(2)}, u32[]{:S(2)}) collective-permute-start(f32[2,1,8,128]{3,2,1,0:T(8,128)} %get-tuple-element.133), channel_id=1, source_target_pairs={{16,0},{32,16},{48,32},{64,48},{80,64},{96,80},{112,96},{128,112},... | collective-permute-start | bytes 24584 | tf_op jit(solution)/shard_map/ppermute | solution.py:19
  205.8 4.2 collective-permute-start.27
  213.0 7.6 %collective-permute-start.29 = (f32[2,6,10,1]{3,2,1,0:T(8,128)S(1)}, f32[2,6,10,1]{3,2,1,0:T(8,128)S(1)}, u32[]{:S(2)}, u32[]{:S(2)}) collective-permute-start(f32[2,6,10,1]{3,2,1,0:T(8,128)S(1)} %get-tuple-element.108), channel_id=1, source_target_pairs={{0,1},{1,2},{2,3},{3,0},{4,5},{5,6},{6,7},{7,4},{8,9},{9,10},{10,1... | collective-permute-start | bytes 1448 | tf_op jit(solution)/shard_map/ppermute | solution.py:16
  223.8 4.2 collective-permute-done.28
  240.4 5.7 %collective-permute-start.31 = (f32[2,1,8,128]{3,2,1,0:T(8,128)S(1)}, f32[2,1,8,128]{3,2,1,0:T(8,128)S(1)}, u32[]{:S(2)}, u32[]{:S(2)}) collective-permute-start(f32[2,1,8,128]{3,2,1,0:T(8,128)S(1)} %get-tuple-element.131), channel_id=1, source_target_pairs={{16,0},{32,16},{48,32},{64,48},{80,64},{96,80},{112,96},{128,112},... | collective-permute-start | bytes 24584 | tf_op jit(solution)/shard_map/ppermute | solution.py:19
  248.8 4.7 %collective-permute-start.33 = (f32[2,6,1,128]{3,2,1,0:T(1,128)S(1)}, f32[2,6,1,128]{3,2,1,0:T(1,128)S(1)}, u32[]{:S(2)}, u32[]{:S(2)}) collective-permute-start(f32[2,6,1,128]{3,2,1,0:T(1,128)S(1)} %get-tuple-element.121), channel_id=1, source_target_pairs={{4,0},{8,4},{12,8},{0,12},{5,1},{9,5},{13,9},{1,13},{6,2},{10,6},{... | collective-permute-start | bytes 18440 | tf_op jit(solution)/shard_map/ppermute | solution.py:19
  254.6 4.1 collective-permute-start.35
  260.7 5.4 %collective-permute-done.34 = f32[2,6,10,1]{3,2,1,0:T(8,128)S(1)} collective-permute-done((f32[2,6,10,1]{3,2,1,0:T(8,128)S(1)}, f32[2,6,10,1]{3,2,1,0:T(8,128)S(1)}, u32[]{:S(2)}, u32[]{:S(2)}) %collective-permute-start.34) | collective-permute-done | bytes 512 | tf_op jit(solution)/shard_map/ppermute | solution.py:19
  278.2 5.6 %collective-permute-start.37 = (f32[2,1,8,128]{3,2,1,0:T(8,128)S(1)}, f32[2,1,8,128]{3,2,1,0:T(8,128)S(1)}, u32[]{:S(2)}, u32[]{:S(2)}) collective-permute-start(f32[2,1,8,128]{3,2,1,0:T(8,128)S(1)} %get-tuple-element.129), channel_id=1, source_target_pairs={{16,0},{32,16},{48,32},{64,48},{80,64},{96,80},{112,96},{128,112},... | collective-permute-start | bytes 24584 | tf_op jit(solution)/shard_map/ppermute | solution.py:19
  284.6 3.2 collective-permute-start.38
  287.7 3.9 collective-permute-start.39
  292.7 4.2 collective-permute-start.41
  298.9 5.4 %collective-permute-done.40 = f32[2,6,10,1]{3,2,1,0:T(8,128)S(1)} collective-permute-done((f32[2,6,10,1]{3,2,1,0:T(8,128)S(1)}, f32[2,6,10,1]{3,2,1,0:T(8,128)S(1)}, u32[]{:S(2)}, u32[]{:S(2)}) %collective-permute-start.40) | collective-permute-done | bytes 512 | tf_op jit(solution)/shard_map/ppermute | solution.py:19
  313.7 5.6 %collective-permute-start.43 = (f32[2,1,8,128]{3,2,1,0:T(8,128)S(1)}, f32[2,1,8,128]{3,2,1,0:T(8,128)S(1)}, u32[]{:S(2)}, u32[]{:S(2)}) collective-permute-start(f32[2,1,8,128]{3,2,1,0:T(8,128)S(1)} %get-tuple-element.127), channel_id=1, source_target_pairs={{16,0},{32,16},{48,32},{64,48},{80,64},{96,80},{112,96},{128,112},... | collective-permute-start | bytes 24584 | tf_op jit(solution)/shard_map/ppermute | solution.py:19
  320.1 3.6 collective-permute-start.44
  323.7 3.1 collective-permute-start.45
  328.2 4.7 %collective-permute-start.47 = (f32[2,6,10,1]{3,2,1,0:T(8,128)S(1)}, f32[2,6,10,1]{3,2,1,0:T(8,128)S(1)}, u32[]{:S(2)}, u32[]{:S(2)}) collective-permute-start(f32[2,6,10,1]{3,2,1,0:T(8,128)S(1)} %get-tuple-element.102), channel_id=1, source_target_pairs={{0,1},{1,2},{2,3},{3,0},{4,5},{5,6},{6,7},{7,4},{8,9},{9,10},{10,1... | collective-permute-start | bytes 1448 | tf_op jit(solution)/shard_map/ppermute | solution.py:16
  334.9 5.4 %collective-permute-done.46 = f32[2,6,10,1]{3,2,1,0:T(8,128)S(1)} collective-permute-done((f32[2,6,10,1]{3,2,1,0:T(8,128)S(1)}, f32[2,6,10,1]{3,2,1,0:T(8,128)S(1)}, u32[]{:S(2)}, u32[]{:S(2)}) %collective-permute-start.46) | collective-permute-done | bytes 512 | tf_op jit(solution)/shard_map/ppermute | solution.py:19
  343.8 104.1 %all-reduce.2 = (f32[]{:T(128)}, f32[64,10]{1,0:T(8,128)S(1)}, f32[64]{0:T(128)S(1)}, f32[64,64]{1,0:T(8,128)S(1)}, f32[64]{0:T(128)S(1)}, /*index=5*/f32[6,64]{1,0:T(8,128)S(1)}, f32[6]{0:T(128)}) all-reduce(f32[]{:T(128)S(6)} %div.30, ...), channel_id=1, replica_groups=mesh['blk'=32,'gy'=4,'rep'=4] {'blk','gy','rep'}, use_global_device_ids=true, to_apply=%region_1.0 | all-reduce | flops 5255 | bytes 42040 | tf_op jit(solution)/shard_map/psum | solution.py:174
  (432 shorter events, 112.5 us)
Async XLA Ops:
  44.3 10.6 %collective-permute-start.1 = (f32[8,1,8,128]{3,2,1,0:T(8,128)S(1)}, f32[8,1,8,128]{3,2,1,0:T(8,128)S(1)}, u32[]{:S(2)}, u32[]{:S(2)}) collective-permute-start(f32[8,1,8,128]{3,2,1,0:T(8,128)S(1)} %get-tuple-element.100), channel_id=1, source_target_pairs={{16,0},{32,16},{48,32},{64,48},{80,64},{96,80},{112,96},{128,112},... | collective-permute-start | bytes 98312 | tf_op jit(solution)/shard_map/ppermute | solution.py:19
  53.0 6.8 %collective-permute-start = (f32[8,1,8,128]{3,2,1,0:T(8,128)S(1)}, f32[8,1,8,128]{3,2,1,0:T(8,128)S(1)}, u32[]{:S(2)}, u32[]{:S(2)}) collective-permute-start(f32[8,1,8,128]{3,2,1,0:T(8,128)S(1)} %get-tuple-element.101), channel_id=1, source_target_pairs={{0,16},{16,32},{32,48},{48,64},{64,80},{80,96},{96,112},{112,128},... | collective-permute-start | bytes 98312 | tf_op jit(solution)/shard_map/ppermute | solution.py:16
  59.8 6.4 %collective-permute-start.3 = (f32[8,6,1,128]{3,2,1,0:T(1,128)S(1)}, f32[8,6,1,128]{3,2,1,0:T(1,128)S(1)}, u32[]{:S(2)}, u32[]{:S(2)}) collective-permute-start(f32[8,6,1,128]{3,2,1,0:T(1,128)S(1)} %get-tuple-element.84), channel_id=1, source_target_pairs={{4,0},{8,4},{12,8},{0,12},{5,1},{9,5},{13,9},{1,13},{6,2},{10,6},{... | collective-permute-start | bytes 73736 | tf_op jit(solution)/shard_map/ppermute | solution.py:19
  64.2 5.8 %collective-permute-start.2 = (f32[8,6,1,128]{3,2,1,0:T(1,128)S(1)}, f32[8,6,1,128]{3,2,1,0:T(1,128)S(1)}, u32[]{:S(2)}, u32[]{:S(2)}) collective-permute-start(f32[8,6,1,128]{3,2,1,0:T(1,128)S(1)} %get-tuple-element.85), channel_id=1, source_target_pairs={{0,4},{4,8},{8,12},{12,0},{1,5},{5,9},{9,13},{13,1},{2,6},{6,10},{... | collective-permute-start | bytes 73736 | tf_op jit(solution)/shard_map/ppermute | solution.py:16
  70.2 13.2 %collective-permute-start.4 = (f32[8,6,10,1]{3,2,1,0:T(8,128)S(1)}, f32[8,6,10,1]{3,2,1,0:T(8,128)S(1)}, u32[]{:S(2)}, u32[]{:S(2)}) collective-permute-start(f32[8,6,10,1]{3,2,1,0:T(8,128)S(1)} %get-tuple-element.64), channel_id=1, source_target_pairs={{1,0},{2,1},{3,2},{0,3},{5,4},{6,5},{7,6},{4,7},{9,8},{10,9},{11,1... | collective-permute-start | bytes 5768 | tf_op jit(solution)/shard_map/ppermute | solution.py:19
  75.2 9.1 %collective-permute-start.5 = (f32[8,6,10,1]{3,2,1,0:T(8,128)S(1)}, f32[8,6,10,1]{3,2,1,0:T(8,128)S(1)}, u32[]{:S(2)}, u32[]{:S(2)}) collective-permute-start(f32[8,6,10,1]{3,2,1,0:T(8,128)S(1)} %get-tuple-element.65), channel_id=1, source_target_pairs={{0,1},{1,2},{2,3},{3,0},{4,5},{5,6},{6,7},{7,4},{8,9},{9,10},{10,1... | collective-permute-start | bytes 5768 | tf_op jit(solution)/shard_map/ppermute | solution.py:16
  87.3 5.3 %collective-permute-start.7 = (f32[8,1,8,128]{3,2,1,0:T(8,128)S(1)}, f32[8,1,8,128]{3,2,1,0:T(8,128)S(1)}, u32[]{:S(2)}, u32[]{:S(2)}) collective-permute-start(f32[8,1,8,128]{3,2,1,0:T(8,128)S(1)} %get-tuple-element.96), channel_id=1, source_target_pairs={{16,0},{32,16},{48,32},{64,48},{80,64},{96,80},{112,96},{128,112},... | collective-permute-start | bytes 98312 | tf_op jit(solution)/shard_map/ppermute | solution.py:19
  89.2 6.8 %collective-permute-start.6 = (f32[8,1,8,128]{3,2,1,0:T(8,128)S(1)}, f32[8,1,8,128]{3,2,1,0:T(8,128)S(1)}, u32[]{:S(2)}, u32[]{:S(2)}) collective-permute-start(f32[8,1,8,128]{3,2,1,0:T(8,128)S(1)} %get-tuple-element.97), channel_id=1, source_target_pairs={{0,16},{16,32},{32,48},{48,64},{64,80},{80,96},{96,112},{112,128},... | collective-permute-start | bytes 98312 | tf_op jit(solution)/shard_map/ppermute | solution.py:16
  96.0 5.4 %collective-permute-start.9 = (f32[8,6,1,128]{3,2,1,0:T(1,128)S(1)}, f32[8,6,1,128]{3,2,1,0:T(1,128)S(1)}, u32[]{:S(2)}, u32[]{:S(2)}) collective-permute-start(f32[8,6,1,128]{3,2,1,0:T(1,128)S(1)} %get-tuple-element.82), channel_id=1, source_target_pairs={{4,0},{8,4},{12,8},{0,12},{5,1},{9,5},{13,9},{1,13},{6,2},{10,6},{... | collective-permute-start | bytes 73736 | tf_op jit(solution)/shard_map/ppermute | solution.py:19
  97.9 5.8 %collective-permute-start.8 = (f32[8,6,1,128]{3,2,1,0:T(1,128)S(1)}, f32[8,6,1,128]{3,2,1,0:T(1,128)S(1)}, u32[]{:S(2)}, u32[]{:S(2)}) collective-permute-start(f32[8,6,1,128]{3,2,1,0:T(1,128)S(1)} %get-tuple-element.83), channel_id=1, source_target_pairs={{0,4},{4,8},{8,12},{12,0},{1,5},{5,9},{9,13},{13,1},{2,6},{6,10},{... | collective-permute-start | bytes 73736 | tf_op jit(solution)/shard_map/ppermute | solution.py:16
  104.0 15.5 %collective-permute-start.10 = (f32[8,6,10,1]{3,2,1,0:T(8,128)S(1)}, f32[8,6,10,1]{3,2,1,0:T(8,128)S(1)}, u32[]{:S(2)}, u32[]{:S(2)}) collective-permute-start(f32[8,6,10,1]{3,2,1,0:T(8,128)S(1)} %get-tuple-element.62), channel_id=1, source_target_pairs={{1,0},{2,1},{3,2},{0,3},{5,4},{6,5},{7,6},{4,7},{9,8},{10,9},{11,1... | collective-permute-start | bytes 5768 | tf_op jit(solution)/shard_map/ppermute | solution.py:19
  110.9 9.1 %collective-permute-start.11 = (f32[8,6,10,1]{3,2,1,0:T(8,128)S(1)}, f32[8,6,10,1]{3,2,1,0:T(8,128)S(1)}, u32[]{:S(2)}, u32[]{:S(2)}) collective-permute-start(f32[8,6,10,1]{3,2,1,0:T(8,128)S(1)} %get-tuple-element.63), channel_id=1, source_target_pairs={{0,1},{1,2},{2,3},{3,0},{4,5},{5,6},{6,7},{7,4},{8,9},{9,10},{10,1... | collective-permute-start | bytes 5768 | tf_op jit(solution)/shard_map/ppermute | solution.py:16
  122.9 5.3 %collective-permute-start.13 = (f32[8,1,8,128]{3,2,1,0:T(8,128)S(1)}, f32[8,1,8,128]{3,2,1,0:T(8,128)S(1)}, u32[]{:S(2)}, u32[]{:S(2)}) collective-permute-start(f32[8,1,8,128]{3,2,1,0:T(8,128)S(1)} %get-tuple-element.92), channel_id=1, source_target_pairs={{16,0},{32,16},{48,32},{64,48},{80,64},{96,80},{112,96},{128,112},... | collective-permute-start | bytes 98312 | tf_op jit(solution)/shard_map/ppermute | solution.py:19
  124.9 6.8 %collective-permute-start.12 = (f32[8,1,8,128]{3,2,1,0:T(8,128)S(1)}, f32[8,1,8,128]{3,2,1,0:T(8,128)S(1)}, u32[]{:S(2)}, u32[]{:S(2)}) collective-permute-start(f32[8,1,8,128]{3,2,1,0:T(8,128)S(1)} %get-tuple-element.93), channel_id=1, source_target_pairs={{0,16},{16,32},{32,48},{48,64},{64,80},{80,96},{96,112},{112,128},... | collective-permute-start | bytes 98312 | tf_op jit(solution)/shard_map/ppermute | solution.py:16
  131.7 5.4 %collective-permute-start.15 = (f32[8,6,1,128]{3,2,1,0:T(1,128)S(1)}, f32[8,6,1,128]{3,2,1,0:T(1,128)S(1)}, u32[]{:S(2)}, u32[]{:S(2)}) collective-permute-start(f32[8,6,1,128]{3,2,1,0:T(1,128)S(1)} %get-tuple-element.80), channel_id=1, source_target_pairs={{4,0},{8,4},{12,8},{0,12},{5,1},{9,5},{13,9},{1,13},{6,2},{10,6},{... | collective-permute-start | bytes 73736 | tf_op jit(solution)/shard_map/ppermute | solution.py:19
  133.6 5.8 %collective-permute-start.14 = (f32[8,6,1,128]{3,2,1,0:T(1,128)S(1)}, f32[8,6,1,128]{3,2,1,0:T(1,128)S(1)}, u32[]{:S(2)}, u32[]{:S(2)}) collective-permute-start(f32[8,6,1,128]{3,2,1,0:T(1,128)S(1)} %get-tuple-element.81), channel_id=1, source_target_pairs={{0,4},{4,8},{8,12},{12,0},{1,5},{5,9},{9,13},{13,1},{2,6},{6,10},{... | collective-permute-start | bytes 73736 | tf_op jit(solution)/shard_map/ppermute | solution.py:16
  139.6 15.3 %collective-permute-start.16 = (f32[8,6,10,1]{3,2,1,0:T(8,128)S(1)}, f32[8,6,10,1]{3,2,1,0:T(8,128)S(1)}, u32[]{:S(2)}, u32[]{:S(2)}) collective-permute-start(f32[8,6,10,1]{3,2,1,0:T(8,128)S(1)} %get-tuple-element.60), channel_id=1, source_target_pairs={{1,0},{2,1},{3,2},{0,3},{5,4},{6,5},{7,6},{4,7},{9,8},{10,9},{11,1... | collective-permute-start | bytes 5768 | tf_op jit(solution)/shard_map/ppermute | solution.py:19
  146.7 9.1 %collective-permute-start.17 = (f32[8,6,10,1]{3,2,1,0:T(8,128)S(1)}, f32[8,6,10,1]{3,2,1,0:T(8,128)S(1)}, u32[]{:S(2)}, u32[]{:S(2)}) collective-permute-start(f32[8,6,10,1]{3,2,1,0:T(8,128)S(1)} %get-tuple-element.61), channel_id=1, source_target_pairs={{0,1},{1,2},{2,3},{3,0},{4,5},{5,6},{6,7},{7,4},{8,9},{9,10},{10,1... | collective-permute-start | bytes 5768 | tf_op jit(solution)/shard_map/ppermute | solution.py:16
  158.5 5.3 %collective-permute-start.19 = (f32[8,1,8,128]{3,2,1,0:T(8,128)S(1)}, f32[8,1,8,128]{3,2,1,0:T(8,128)S(1)}, u32[]{:S(2)}, u32[]{:S(2)}) collective-permute-start(f32[8,1,8,128]{3,2,1,0:T(8,128)S(1)} %get-tuple-element.88), channel_id=1, source_target_pairs={{16,0},{32,16},{48,32},{64,48},{80,64},{96,80},{112,96},{128,112},... | collective-permute-start | bytes 98312 | tf_op jit(solution)/shard_map/ppermute | solution.py:19
  160.4 6.8 %collective-permute-start.18 = (f32[8,1,8,128]{3,2,1,0:T(8,128)S(1)}, f32[8,1,8,128]{3,2,1,0:T(8,128)S(1)}, u32[]{:S(2)}, u32[]{:S(2)}) collective-permute-start(f32[8,1,8,128]{3,2,1,0:T(8,128)S(1)} %get-tuple-element.89), channel_id=1, source_target_pairs={{0,16},{16,32},{32,48},{48,64},{64,80},{80,96},{96,112},{112,128},... | collective-permute-start | bytes 98312 | tf_op jit(solution)/shard_map/ppermute | solution.py:16
  167.2 5.4 %collective-permute-start.21 = (f32[8,6,1,128]{3,2,1,0:T(1,128)S(1)}, f32[8,6,1,128]{3,2,1,0:T(1,128)S(1)}, u32[]{:S(2)}, u32[]{:S(2)}) collective-permute-start(f32[8,6,1,128]{3,2,1,0:T(1,128)S(1)} %get-tuple-element.78), channel_id=1, source_target_pairs={{4,0},{8,4},{12,8},{0,12},{5,1},{9,5},{13,9},{1,13},{6,2},{10,6},{... | collective-permute-start | bytes 73736 | tf_op jit(solution)/shard_map/ppermute | solution.py:19
  169.2 5.8 %collective-permute-start.20 = (f32[8,6,1,128]{3,2,1,0:T(1,128)S(1)}, f32[8,6,1,128]{3,2,1,0:T(1,128)S(1)}, u32[]{:S(2)}, u32[]{:S(2)}) collective-permute-start(f32[8,6,1,128]{3,2,1,0:T(1,128)S(1)} %get-tuple-element.79), channel_id=1, source_target_pairs={{0,4},{4,8},{8,12},{12,0},{1,5},{5,9},{9,13},{13,1},{2,6},{6,10},{... | collective-permute-start | bytes 73736 | tf_op jit(solution)/shard_map/ppermute | solution.py:16
  175.2 15.7 %collective-permute-start.22 = (f32[8,6,10,1]{3,2,1,0:T(8,128)S(1)}, f32[8,6,10,1]{3,2,1,0:T(8,128)S(1)}, u32[]{:S(2)}, u32[]{:S(2)}) collective-permute-start(f32[8,6,10,1]{3,2,1,0:T(8,128)S(1)} %get-tuple-element.58), channel_id=1, source_target_pairs={{1,0},{2,1},{3,2},{0,3},{5,4},{6,5},{7,6},{4,7},{9,8},{10,9},{11,1... | collective-permute-start | bytes 5768 | tf_op jit(solution)/shard_map/ppermute | solution.py:19
  182.3 9.1 %collective-permute-start.23 = (f32[8,6,10,1]{3,2,1,0:T(8,128)S(1)}, f32[8,6,10,1]{3,2,1,0:T(8,128)S(1)}, u32[]{:S(2)}, u32[]{:S(2)}) collective-permute-start(f32[8,6,10,1]{3,2,1,0:T(8,128)S(1)} %get-tuple-element.59), channel_id=1, source_target_pairs={{0,1},{1,2},{2,3},{3,0},{4,5},{5,6},{6,7},{7,4},{8,9},{9,10},{10,1... | collective-permute-start | bytes 5768 | tf_op jit(solution)/shard_map/ppermute | solution.py:16
  193.7 7.4 %collective-permute-start.24 = (f32[2,1,8,128]{3,2,1,0:T(8,128)}, f32[2,1,8,128]{3,2,1,0:T(8,128)S(1)}, u32[]{:S(2)}, u32[]{:S(2)}) collective-permute-start(f32[2,1,8,128]{3,2,1,0:T(8,128)} %get-tuple-element.132), channel_id=1, source_target_pairs={{0,16},{16,32},{32,48},{48,64},{64,80},{80,96},{96,112},{112,128},... | collective-permute-start | bytes 24584 | tf_op jit(solution)/shard_map/ppermute | solution.py:16
  195.6 6.5 %collective-permute-start.25 = (f32[2,1,8,128]{3,2,1,0:T(8,128)}, f32[2,1,8,128]{3,2,1,0:T(8,128)}, u32[]{:S(2)}, u32[]{:S(2)}) collective-permute-start(f32[2,1,8,128]{3,2,1,0:T(8,128)} %get-tuple-element.133), channel_id=1, source_target_pairs={{16,0},{32,16},{48,32},{64,48},{80,64},{96,80},{112,96},{128,112},... | collective-permute-start | bytes 24584 | tf_op jit(solution)/shard_map/ppermute | solution.py:19
  203.5 8.5 %collective-permute-start.26 = (f32[2,6,1,128]{3,2,1,0:T(1,128)}, f32[2,6,1,128]{3,2,1,0:T(1,128)}, u32[]{:S(2)}, u32[]{:S(2)}) collective-permute-start(f32[2,6,1,128]{3,2,1,0:T(1,128)} %get-tuple-element.124), channel_id=1, source_target_pairs={{0,4},{4,8},{8,12},{12,0},{1,5},{5,9},{9,13},{13,1},{2,6},{6,10},{... | collective-permute-start | bytes 18440 | tf_op jit(solution)/shard_map/ppermute | solution.py:16
  205.8 6.3 %collective-permute-start.27 = (f32[2,6,1,128]{3,2,1,0:T(1,128)}, f32[2,6,1,128]{3,2,1,0:T(1,128)}, u32[]{:S(2)}, u32[]{:S(2)}) collective-permute-start(f32[2,6,1,128]{3,2,1,0:T(1,128)} %get-tuple-element.125), channel_id=1, source_target_pairs={{4,0},{8,4},{12,8},{0,12},{5,1},{9,5},{13,9},{1,13},{6,2},{10,6},{... | collective-permute-start | bytes 18440 | tf_op jit(solution)/shard_map/ppermute | solution.py:19
  213.0 10.8 %collective-permute-start.29 = (f32[2,6,10,1]{3,2,1,0:T(8,128)S(1)}, f32[2,6,10,1]{3,2,1,0:T(8,128)S(1)}, u32[]{:S(2)}, u32[]{:S(2)}) collective-permute-start(f32[2,6,10,1]{3,2,1,0:T(8,128)S(1)} %get-tuple-element.108), channel_id=1, source_target_pairs={{0,1},{1,2},{2,3},{3,0},{4,5},{5,6},{6,7},{7,4},{8,9},{9,10},{10,1... | collective-permute-start | bytes 1448 | tf_op jit(solution)/shard_map/ppermute | solution.py:16
  220.6 7.4 %collective-permute-start.28 = (f32[2,6,10,1]{3,2,1,0:T(8,128)S(1)}, f32[2,6,10,1]{3,2,1,0:T(8,128)S(1)}, u32[]{:S(2)}, u32[]{:S(2)}) collective-permute-start(f32[2,6,10,1]{3,2,1,0:T(8,128)S(1)} %get-tuple-element.109), channel_id=1, source_target_pairs={{1,0},{2,1},{3,2},{0,3},{5,4},{6,5},{7,6},{4,7},{9,8},{10,9},{11,1... | collective-permute-start | bytes 1448 | tf_op jit(solution)/shard_map/ppermute | solution.py:19
  238.5 7.9 %collective-permute-start.30 = (f32[2,1,8,128]{3,2,1,0:T(8,128)S(1)}, f32[2,1,8,128]{3,2,1,0:T(8,128)S(1)}, u32[]{:S(2)}, u32[]{:S(2)}) collective-permute-start(f32[2,1,8,128]{3,2,1,0:T(8,128)S(1)} %get-tuple-element.130), channel_id=1, source_target_pairs={{0,16},{16,32},{32,48},{48,64},{64,80},{80,96},{96,112},{112,128},... | collective-permute-start | bytes 24584 | tf_op jit(solution)/shard_map/ppermute | solution.py:16
  240.4 6.4 %collective-permute-start.31 = (f32[2,1,8,128]{3,2,1,0:T(8,128)S(1)}, f32[2,1,8,128]{3,2,1,0:T(8,128)S(1)}, u32[]{:S(2)}, u32[]{:S(2)}) collective-permute-start(f32[2,1,8,128]{3,2,1,0:T(8,128)S(1)} %get-tuple-element.131), channel_id=1, source_target_pairs={{16,0},{32,16},{48,32},{64,48},{80,64},{96,80},{112,96},{128,112},... | collective-permute-start | bytes 24584 | tf_op jit(solution)/shard_map/ppermute | solution.py:19
  246.9 7.5 %collective-permute-start.32 = (f32[2,6,1,128]{3,2,1,0:T(1,128)S(1)}, f32[2,6,1,128]{3,2,1,0:T(1,128)S(1)}, u32[]{:S(2)}, u32[]{:S(2)}) collective-permute-start(f32[2,6,1,128]{3,2,1,0:T(1,128)S(1)} %get-tuple-element.120), channel_id=1, source_target_pairs={{0,4},{4,8},{8,12},{12,0},{1,5},{5,9},{9,13},{13,1},{2,6},{6,10},{... | collective-permute-start | bytes 18440 | tf_op jit(solution)/shard_map/ppermute | solution.py:16
  248.8 5.6 %collective-permute-start.33 = (f32[2,6,1,128]{3,2,1,0:T(1,128)S(1)}, f32[2,6,1,128]{3,2,1,0:T(1,128)S(1)}, u32[]{:S(2)}, u32[]{:S(2)}) collective-permute-start(f32[2,6,1,128]{3,2,1,0:T(1,128)S(1)} %get-tuple-element.121), channel_id=1, source_target_pairs={{4,0},{8,4},{12,8},{0,12},{5,1},{9,5},{13,9},{1,13},{6,2},{10,6},{... | collective-permute-start | bytes 18440 | tf_op jit(solution)/shard_map/ppermute | solution.py:19
  254.6 6.1 %collective-permute-start.35 = (f32[2,6,10,1]{3,2,1,0:T(8,128)S(1)}, f32[2,6,10,1]{3,2,1,0:T(8,128)S(1)}, u32[]{:S(2)}, u32[]{:S(2)}) collective-permute-start(f32[2,6,10,1]{3,2,1,0:T(8,128)S(1)} %get-tuple-element.106), channel_id=1, source_target_pairs={{0,1},{1,2},{2,3},{3,0},{4,5},{5,6},{6,7},{7,4},{8,9},{9,10},{10,1... | collective-permute-start | bytes 1448 | tf_op jit(solution)/shard_map/ppermute | solution.py:16
  258.7 7.4 %collective-permute-start.34 = (f32[2,6,10,1]{3,2,1,0:T(8,128)S(1)}, f32[2,6,10,1]{3,2,1,0:T(8,128)S(1)}, u32[]{:S(2)}, u32[]{:S(2)}) collective-permute-start(f32[2,6,10,1]{3,2,1,0:T(8,128)S(1)} %get-tuple-element.107), channel_id=1, source_target_pairs={{1,0},{2,1},{3,2},{0,3},{5,4},{6,5},{7,6},{4,7},{9,8},{10,9},{11,1... | collective-permute-start | bytes 1448 | tf_op jit(solution)/shard_map/ppermute | solution.py:19
  276.2 7.8 %collective-permute-start.36 = (f32[2,1,8,128]{3,2,1,0:T(8,128)S(1)}, f32[2,1,8,128]{3,2,1,0:T(8,128)S(1)}, u32[]{:S(2)}, u32[]{:S(2)}) collective-permute-start(f32[2,1,8,128]{3,2,1,0:T(8,128)S(1)} %get-tuple-element.128), channel_id=1, source_target_pairs={{0,16},{16,32},{32,48},{48,64},{64,80},{80,96},{96,112},{112,128},... | collective-permute-start | bytes 24584 | tf_op jit(solution)/shard_map/ppermute | solution.py:16
  278.2 6.4 %collective-permute-start.37 = (f32[2,1,8,128]{3,2,1,0:T(8,128)S(1)}, f32[2,1,8,128]{3,2,1,0:T(8,128)S(1)}, u32[]{:S(2)}, u32[]{:S(2)}) collective-permute-start(f32[2,1,8,128]{3,2,1,0:T(8,128)S(1)} %get-tuple-element.129), channel_id=1, source_target_pairs={{16,0},{32,16},{48,32},{64,48},{80,64},{96,80},{112,96},{128,112},... | collective-permute-start | bytes 24584 | tf_op jit(solution)/shard_map/ppermute | solution.py:19
  284.6 8.0 %collective-permute-start.38 = (f32[2,6,1,128]{3,2,1,0:T(1,128)S(1)}, f32[2,6,1,128]{3,2,1,0:T(1,128)S(1)}, u32[]{:S(2)}, u32[]{:S(2)}) collective-permute-start(f32[2,6,1,128]{3,2,1,0:T(1,128)S(1)} %get-tuple-element.116), channel_id=1, source_target_pairs={{0,4},{4,8},{8,12},{12,0},{1,5},{5,9},{9,13},{13,1},{2,6},{6,10},{... | collective-permute-start | bytes 18440 | tf_op jit(solution)/shard_map/ppermute | solution.py:16
  287.7 4.8 %collective-permute-start.39 = (f32[2,6,1,128]{3,2,1,0:T(1,128)S(1)}, f32[2,6,1,128]{3,2,1,0:T(1,128)S(1)}, u32[]{:S(2)}, u32[]{:S(2)}) collective-permute-start(f32[2,6,1,128]{3,2,1,0:T(1,128)S(1)} %get-tuple-element.117), channel_id=1, source_target_pairs={{4,0},{8,4},{12,8},{0,12},{5,1},{9,5},{13,9},{1,13},{6,2},{10,6},{... | collective-permute-start | bytes 18440 | tf_op jit(solution)/shard_map/ppermute | solution.py:19
  292.7 6.2 %collective-permute-start.41 = (f32[2,6,10,1]{3,2,1,0:T(8,128)S(1)}, f32[2,6,10,1]{3,2,1,0:T(8,128)S(1)}, u32[]{:S(2)}, u32[]{:S(2)}) collective-permute-start(f32[2,6,10,1]{3,2,1,0:T(8,128)S(1)} %get-tuple-element.104), channel_id=1, source_target_pairs={{0,1},{1,2},{2,3},{3,0},{4,5},{5,6},{6,7},{7,4},{8,9},{9,10},{10,1... | collective-permute-start | bytes 1448 | tf_op jit(solution)/shard_map/ppermute | solution.py:16
  296.9 7.4 %collective-permute-start.40 = (f32[2,6,10,1]{3,2,1,0:T(8,128)S(1)}, f32[2,6,10,1]{3,2,1,0:T(8,128)S(1)}, u32[]{:S(2)}, u32[]{:S(2)}) collective-permute-start(f32[2,6,10,1]{3,2,1,0:T(8,128)S(1)} %get-tuple-element.105), channel_id=1, source_target_pairs={{1,0},{2,1},{3,2},{0,3},{5,4},{6,5},{7,6},{4,7},{9,8},{10,9},{11,1... | collective-permute-start | bytes 1448 | tf_op jit(solution)/shard_map/ppermute | solution.py:19
  311.7 7.8 %collective-permute-start.42 = (f32[2,1,8,128]{3,2,1,0:T(8,128)S(1)}, f32[2,1,8,128]{3,2,1,0:T(8,128)S(1)}, u32[]{:S(2)}, u32[]{:S(2)}) collective-permute-start(f32[2,1,8,128]{3,2,1,0:T(8,128)S(1)} %get-tuple-element.126), channel_id=1, source_target_pairs={{0,16},{16,32},{32,48},{48,64},{64,80},{80,96},{96,112},{112,128},... | collective-permute-start | bytes 24584 | tf_op jit(solution)/shard_map/ppermute | solution.py:16
  313.7 6.4 %collective-permute-start.43 = (f32[2,1,8,128]{3,2,1,0:T(8,128)S(1)}, f32[2,1,8,128]{3,2,1,0:T(8,128)S(1)}, u32[]{:S(2)}, u32[]{:S(2)}) collective-permute-start(f32[2,1,8,128]{3,2,1,0:T(8,128)S(1)} %get-tuple-element.127), channel_id=1, source_target_pairs={{16,0},{32,16},{48,32},{64,48},{80,64},{96,80},{112,96},{128,112},... | collective-permute-start | bytes 24584 | tf_op jit(solution)/shard_map/ppermute | solution.py:19
  320.1 7.7 %collective-permute-start.44 = (f32[2,6,1,128]{3,2,1,0:T(1,128)S(1)}, f32[2,6,1,128]{3,2,1,0:T(1,128)S(1)}, u32[]{:S(2)}, u32[]{:S(2)}) collective-permute-start(f32[2,6,1,128]{3,2,1,0:T(1,128)S(1)} %get-tuple-element.112), channel_id=1, source_target_pairs={{0,4},{4,8},{8,12},{12,0},{1,5},{5,9},{9,13},{13,1},{2,6},{6,10},{... | collective-permute-start | bytes 18440 | tf_op jit(solution)/shard_map/ppermute | solution.py:16
  323.7 4.4 collective-permute-start.45
  328.2 6.7 %collective-permute-start.47 = (f32[2,6,10,1]{3,2,1,0:T(8,128)S(1)}, f32[2,6,10,1]{3,2,1,0:T(8,128)S(1)}, u32[]{:S(2)}, u32[]{:S(2)}) collective-permute-start(f32[2,6,10,1]{3,2,1,0:T(8,128)S(1)} %get-tuple-element.102), channel_id=1, source_target_pairs={{0,1},{1,2},{2,3},{3,0},{4,5},{5,6},{6,7},{7,4},{8,9},{9,10},{10,1... | collective-permute-start | bytes 1448 | tf_op jit(solution)/shard_map/ppermute | solution.py:16
  332.9 7.4 %collective-permute-start.46 = (f32[2,6,10,1]{3,2,1,0:T(8,128)S(1)}, f32[2,6,10,1]{3,2,1,0:T(8,128)S(1)}, u32[]{:S(2)}, u32[]{:S(2)}) collective-permute-start(f32[2,6,10,1]{3,2,1,0:T(8,128)S(1)} %get-tuple-element.103), channel_id=1, source_target_pairs={{1,0},{2,1},{3,2},{0,3},{5,4},{6,5},{7,6},{4,7},{9,8},{10,9},{11,1... | collective-permute-start | bytes 1448 | tf_op jit(solution)/shard_map/ppermute | solution.py:19
  (111 other events, 1441.8 us)
where the time goes:
time: 456 us; the launch traced here: 452 us
  starting transfers between devices  174 us (38%)
  blocking collectives  138 us (30%)
  waiting for transfers between devices  71.5 us (16%)
  other arithmetic  25.7 us (6%)
  matrix products  21.9 us (5%)
  local copies, waits for them, and re-layouts  17.4 us (4%)
    psum x1, blocking collectives, per_device(): lax.psum((sum_w_in, sum_b_in, sum_w_mid, sum_b_mid, sum_w_out, sum_b_out,...  104 us
    ppermute x24, starting transfers between devices, extended(): lax.ppermute(lax.slice_in_dim(block, 0, width, axis=dim), axis, backward)  96.7 us
    ppermute x24, starting transfers between devices, extended(): lax.ppermute(lax.slice_in_dim(block, block.shape[dim] - width, None, axis...  77 us
    ppermute x24, waiting for transfers between devices, extended(): lax.ppermute(lax.slice_in_dim(block, 0, width, axis=dim), axis, backward)  43.1 us
    ppermute x24, waiting for transfers between devices, extended(): lax.ppermute(lax.slice_in_dim(block, block.shape[dim] - width, None, axis...  28.4 us
    unnamed x1, blocking collectives  13.4 us
  transfers between devices with their start and end apart: 48, of which 25 were waited for; matrix products, arithmetic and copies ran while one was open for 1% of the time, Pallas kernels for 0%

commit v1 on v0

--- a/solution.py
+++ b/solution.py
@@ -5,6 +5,11 @@
 
 STEPS = 4
 RATE_MAX = 0.15
+
+
+def axis_by_axis(array, one, other):
+    half = lax.psum(array, one)
+    return lax.psum(half, other)
 
 
 def extended(block, sides, width):
@@ -171,9 +176,10 @@
         )
     start_sensitivity = adjoint * (2.0 * total_cells)
     sum_w_in, sum_b_in, sum_w_mid, sum_b_mid, sum_w_out, sum_b_out = grad_sums
-    summed = lax.psum(
+    summed = axis_by_axis(
         (sum_w_in, sum_b_in, sum_w_mid, sum_b_mid, sum_w_out, sum_b_out, loss_part),
-        ("blk", "gy", "rep"),
+        ("gy", "rep"),
+        "blk",
     )
     position = lax.axis_index("rep")
     share_width = w_in.shape[0]

time: 456 us -> 542 us (1.19)
  the two profiles are of different devices: /device:TPU:1 before, /device:TPU:8 now
where the time goes in v1:
time: 542 us; the launch traced here: 539 us
  blocking collectives  223 us (41%)
  starting transfers between devices  163 us (30%)
  waiting for transfers between devices  83.6 us (15%)
  other arithmetic  25.6 us (5%)
  matrix products  22 us (4%)
  local copies, waits for them, and re-layouts  17.4 us (3%)
    psum x1, blocking collectives, axis_by_axis(): return lax.psum(half, other)  123 us
    ppermute x24, starting transfers between devices, extended(): lax.ppermute(lax.slice_in_dim(block, 0, width, axis=dim), axis, backward)  99.5 us
    psum x1, blocking collectives, axis_by_axis(): half = lax.psum(array, one)  71.4 us
    ppermute x24, starting transfers between devices, extended(): lax.ppermute(lax.slice_in_dim(block, block.shape[dim] - width, None, axis...  63.6 us
    ppermute x24, waiting for transfers between devices, extended(): lax.ppermute(lax.slice_in_dim(block, block.shape[dim] - width, None, axis...  54 us
    ppermute x24, waiting for transfers between devices, extended(): lax.ppermute(lax.slice_in_dim(block, 0, width, axis=dim), axis, backward)  29.7 us
  transfers between devices with their start and end apart: 48, of which 30 were waited for; matrix products, arithmetic and copies ran while one was open for 1% of the time, Pallas kernels for 0%

profile of v1, /device:TPU:8, one launch (start us, length us, event | category | flops | bytes accessed | tf_op | source)
XLA Modules:
  0.0 539.4 jit_solution(2868343613934609087)
XLA Ops:
  5.0 9.2 %all-reduce.4 = (bf16[64]{0:T(256)(128)(2,1)S(1)}, bf16[64]{0:T(256)(128)(2,1)S(1)}) all-reduce(bf16[64]{0:T(256)(128)(2,1)S(1)} %dynamic-update-slice.1, bf16[64]{0:T(256)(128)(2,1)S(1)} %dynamic-update-slice), channel_id=1, replica_groups=mesh['blk'=32,'gy'=4,'rep'=4] {'rep'}, use_global_device_ids=true, to_apply=%add.1 | all-reduce | flops 128 | bytes 512
  16.3 6.7 %all-gather = bf16[4,16,6]{1,2,0:T(8,128)(2,1)S(1)} all-gather(bf16[1,16,6]{1,2,0:T(8,128)(2,1)S(1)} %convert_bitcast_fusion.4), channel_id=1, replica_groups=mesh['blk'=32,'gy'=4,'rep'=4] {'rep'}, dimensions={0}, use_global_device_ids=true | all-gather | bytes 960 | tf_op jit(solution)/shard_map/all_gather | solution.py:128
  23.1 6.7 %all_gather.17 = bf16[64,64]{1,0:T(8,128)(2,1)S(1)} all-gather(bf16[16,64]{1,0:T(8,128)(2,1)S(1)} %convert_element_type.210), channel_id=1, replica_groups=mesh['blk'=32,'gy'=4,'rep'=4] {'rep'}, dimensions={0}, use_global_device_ids=true | all-gather | bytes 10240 | tf_op jit(solution)/shard_map/all_gather | solution.py:126
  29.7 6.7 %all_gather.15 = bf16[64,10]{1,0:T(8,128)(2,1)S(1)} all-gather(bf16[16,10]{1,0:T(8,128)(2,1)S(1)} %convert_element_type.206), channel_id=1, replica_groups=mesh['blk'=32,'gy'=4,'rep'=4] {'rep'}, dimensions={0}, use_global_device_ids=true | all-gather | bytes 1600 | tf_op jit(solution)/shard_map/all_gather | solution.py:124
  39.5 12.2 %collective-permute-start.1 = (f32[8,1,8,128]{3,2,1,0:T(8,128)S(1)}, f32[8,1,8,128]{3,2,1,0:T(8,128)S(1)}, u32[]{:S(2)}, u32[]{:S(2)}) collective-permute-start(f32[8,1,8,128]{3,2,1,0:T(8,128)S(1)} %get-tuple-element.107), channel_id=1, source_target_pairs={{16,0},{32,16},{48,32},{64,48},{80,64},{96,80},{112,96},{128,112},... | collective-permute-start | bytes 98312 | tf_op jit(solution)/shard_map/ppermute | solution.py:24
  53.7 6.0 %collective-permute-done = f32[8,1,8,128]{3,2,1,0:T(8,128)S(1)} collective-permute-done((f32[8,1,8,128]{3,2,1,0:T(8,128)S(1)}, f32[8,1,8,128]{3,2,1,0:T(8,128)S(1)}, u32[]{:S(2)}, u32[]{:S(2)}) %collective-permute-start) | collective-permute-done | bytes 32800 | tf_op jit(solution)/shard_map/ppermute | solution.py:21
  59.7 4.7 collective-permute-start.3
  66.4 4.9 collective-permute-done.2
  73.5 2.4 collective-permute-start.5
  75.9 5.1 collective-permute-done.4
  81.0 3.1 collective-permute-done.5
  88.9 3.9 collective-permute-start.6
  92.9 4.0 collective-permute-done.6
  98.8 3.9 collective-permute-start.8
  102.8 2.9 collective-permute-done.8
  107.9 2.4 collective-permute-start.11
  110.4 2.8 collective-permute-done.10
  113.2 7.5 %collective-permute-done.11 = f32[8,6,10,1]{3,2,1,0:T(8,128)S(1)} collective-permute-done((f32[8,6,10,1]{3,2,1,0:T(8,128)S(1)}, f32[8,6,10,1]{3,2,1,0:T(8,128)S(1)}, u32[]{:S(2)}, u32[]{:S(2)}) %collective-permute-start.11) | collective-permute-done | bytes 1952 | tf_op jit(solution)/shard_map/ppermute | solution.py:21
  125.9 3.6 collective-permute-start.12
  129.6 4.3 collective-permute-done.12
  135.8 3.9 collective-permute-start.14
  139.8 2.9 collective-permute-done.14
  144.9 2.4 collective-permute-start.17
  147.4 5.2 collective-permute-done.16
  152.6 2.9 collective-permute-done.17
  160.1 3.9 collective-permute-start.18
  164.1 4.0 collective-permute-done.18
  170.2 3.7 collective-permute-start.20
  174.0 3.1 collective-permute-done.20
  181.8 2.8 collective-permute-done.22
  184.6 7.5 %collective-permute-done.23 = f32[8,6,10,1]{3,2,1,0:T(8,128)S(1)} collective-permute-done((f32[8,6,10,1]{3,2,1,0:T(8,128)S(1)}, f32[8,6,10,1]{3,2,1,0:T(8,128)S(1)}, u32[]{:S(2)}, u32[]{:S(2)}) %collective-permute-start.23) | collective-permute-done | bytes 1952 | tf_op jit(solution)/shard_map/ppermute | solution.py:21
  196.3 6.0 %collective-permute-start.25 = (f32[2,1,8,128]{3,2,1,0:T(8,128)}, f32[2,1,8,128]{3,2,1,0:T(8,128)}, u32[]{:S(2)}, u32[]{:S(2)}) collective-permute-start(f32[2,1,8,128]{3,2,1,0:T(8,128)} %get-tuple-element.140), channel_id=1, source_target_pairs={{16,0},{32,16},{48,32},{64,48},{80,64},{96,80},{112,96},{128,112},... | collective-permute-start | bytes 24584 | tf_op jit(solution)/shard_map/ppermute | solution.py:24
  205.4 2.5 collective-permute-start.26
  207.9 4.5 collective-permute-start.27
  217.3 5.3 collective-permute-start.28
  237.2 6.6 %collective-permute-start.31 = (f32[2,1,8,128]{3,2,1,0:T(8,128)S(1)}, f32[2,1,8,128]{3,2,1,0:T(8,128)S(1)}, u32[]{:S(2)}, u32[]{:S(2)}) collective-permute-start(f32[2,1,8,128]{3,2,1,0:T(8,128)S(1)} %get-tuple-element.138), channel_id=1, source_target_pairs={{16,0},{32,16},{48,32},{64,48},{80,64},{96,80},{112,96},{128,112},... | collective-permute-start | bytes 24584 | tf_op jit(solution)/shard_map/ppermute | solution.py:24
  247.0 5.1 collective-permute-start.33
  255.5 5.1 collective-permute-start.34
  274.9 6.4 %collective-permute-start.37 = (f32[2,1,8,128]{3,2,1,0:T(8,128)S(1)}, f32[2,1,8,128]{3,2,1,0:T(8,128)S(1)}, u32[]{:S(2)}, u32[]{:S(2)}) collective-permute-start(f32[2,1,8,128]{3,2,1,0:T(8,128)S(1)} %get-tuple-element.136), channel_id=1, source_target_pairs={{16,0},{32,16},{48,32},{64,48},{80,64},{96,80},{112,96},{128,112},... | collective-permute-start | bytes 24584 | tf_op jit(solution)/shard_map/ppermute | solution.py:24
  282.7 3.4 collective-permute-start.38
  286.1 3.9 collective-permute-start.39
  293.7 5.1 collective-permute-start.40
  310.4 6.4 %collective-permute-start.43 = (f32[2,1,8,128]{3,2,1,0:T(8,128)S(1)}, f32[2,1,8,128]{3,2,1,0:T(8,128)S(1)}, u32[]{:S(2)}, u32[]{:S(2)}) collective-permute-start(f32[2,1,8,128]{3,2,1,0:T(8,128)S(1)} %get-tuple-element.134), channel_id=1, source_target_pairs={{16,0},{32,16},{48,32},{64,48},{80,64},{96,80},{112,96},{128,112},... | collective-permute-start | bytes 24584 | tf_op jit(solution)/shard_map/ppermute | solution.py:24
  318.2 3.9 collective-permute-start.44
  322.1 3.1 collective-permute-start.45
  329.7 5.1 collective-permute-start.46
  340.5 71.4 %all-reduce.3 = (f32[]{:T(128)}, f32[64,10]{1,0:T(8,128)S(1)}, f32[64]{0:T(128)S(1)}, f32[64,64]{1,0:T(8,128)S(1)}, f32[64]{0:T(128)S(1)}, /*index=5*/f32[6,64]{1,0:T(8,128)S(1)}, f32[6]{0:T(128)S(1)}) all-reduce(f32[]{:T(128)S(6)} %div.30, ...), channel_id=1, replica_groups=mesh['blk'=32,'gy'=4,'rep'=4] {'gy','rep'}, use_global_device_ids=true, to_apply=%region_1.0 | all-reduce | flops 5255 | bytes 42040 | tf_op jit(solution)/shard_map/psum | solution.py:11
  411.9 122.8 %all-reduce.2 = (f32[]{:T(128)}, f32[64,10]{1,0:T(8,128)S(1)}, f32[64]{0:T(128)S(1)}, f32[64,64]{1,0:T(8,128)S(1)}, f32[64]{0:T(128)S(1)}, /*index=5*/f32[6,64]{1,0:T(8,128)S(1)}, f32[6]{0:T(128)}) all-reduce(f32[]{:T(128)} %get-tuple-element.16, ...), channel_id=1, replica_groups=mesh['blk'=32,'gy'=4,'rep'=4] {'blk'}, use_global_device_ids=true, to_apply=%region_2.0 | all-reduce | flops 5255 | bytes 42040 | tf_op jit(solution)/shard_map/psum | solution.py:12
  (433 shorter events, 122.9 us)
Async XLA Ops:
  39.5 14.1 %collective-permute-start.1 = (f32[8,1,8,128]{3,2,1,0:T(8,128)S(1)}, f32[8,1,8,128]{3,2,1,0:T(8,128)S(1)}, u32[]{:S(2)}, u32[]{:S(2)}) collective-permute-start(f32[8,1,8,128]{3,2,1,0:T(8,128)S(1)} %get-tuple-element.107), channel_id=1, source_target_pairs={{16,0},{32,16},{48,32},{64,48},{80,64},{96,80},{112,96},{128,112},... | collective-permute-start | bytes 98312 | tf_op jit(solution)/shard_map/ppermute | solution.py:24
  51.7 7.9 %collective-permute-start = (f32[8,1,8,128]{3,2,1,0:T(8,128)S(1)}, f32[8,1,8,128]{3,2,1,0:T(8,128)S(1)}, u32[]{:S(2)}, u32[]{:S(2)}) collective-permute-start(f32[8,1,8,128]{3,2,1,0:T(8,128)S(1)} %get-tuple-element.108), channel_id=1, source_target_pairs={{0,16},{16,32},{32,48},{48,64},{64,80},{80,96},{96,112},{112,128},... | collective-permute-start | bytes 98312 | tf_op jit(solution)/shard_map/ppermute | solution.py:21
  59.7 6.7 %collective-permute-start.3 = (f32[8,6,1,128]{3,2,1,0:T(1,128)S(1)}, f32[8,6,1,128]{3,2,1,0:T(1,128)S(1)}, u32[]{:S(2)}, u32[]{:S(2)}) collective-permute-start(f32[8,6,1,128]{3,2,1,0:T(1,128)S(1)} %get-tuple-element.91), channel_id=1, source_target_pairs={{4,0},{8,4},{12,8},{0,12},{5,1},{9,5},{13,9},{1,13},{6,2},{10,6},{... | collective-permute-start | bytes 73736 | tf_op jit(solution)/shard_map/ppermute | solution.py:24
  64.4 6.9 %collective-permute-start.2 = (f32[8,6,1,128]{3,2,1,0:T(1,128)S(1)}, f32[8,6,1,128]{3,2,1,0:T(1,128)S(1)}, u32[]{:S(2)}, u32[]{:S(2)}) collective-permute-start(f32[8,6,1,128]{3,2,1,0:T(1,128)S(1)} %get-tuple-element.92), channel_id=1, source_target_pairs={{0,4},{4,8},{8,12},{12,0},{1,5},{5,9},{9,13},{13,1},{2,6},{6,10},{... | collective-permute-start | bytes 73736 | tf_op jit(solution)/shard_map/ppermute | solution.py:21
  71.6 9.4 %collective-permute-start.4 = (f32[8,6,10,1]{3,2,1,0:T(8,128)S(1)}, f32[8,6,10,1]{3,2,1,0:T(8,128)S(1)}, u32[]{:S(2)}, u32[]{:S(2)}) collective-permute-start(f32[8,6,10,1]{3,2,1,0:T(8,128)S(1)} %get-tuple-element.71), channel_id=1, source_target_pairs={{1,0},{2,1},{3,2},{0,3},{5,4},{6,5},{7,6},{4,7},{9,8},{10,9},{11,1... | collective-permute-start | bytes 5768 | tf_op jit(solution)/shard_map/ppermute | solution.py:24
  73.5 10.6 %collective-permute-start.5 = (f32[8,6,10,1]{3,2,1,0:T(8,128)S(1)}, f32[8,6,10,1]{3,2,1,0:T(8,128)S(1)}, u32[]{:S(2)}, u32[]{:S(2)}) collective-permute-start(f32[8,6,10,1]{3,2,1,0:T(8,128)S(1)} %get-tuple-element.72), channel_id=1, source_target_pairs={{0,1},{1,2},{2,3},{3,0},{4,5},{5,6},{6,7},{7,4},{8,9},{9,10},{10,1... | collective-permute-start | bytes 5768 | tf_op jit(solution)/shard_map/ppermute | solution.py:21
  87.0 5.9 %collective-permute-start.7 = (f32[8,1,8,128]{3,2,1,0:T(8,128)S(1)}, f32[8,1,8,128]{3,2,1,0:T(8,128)S(1)}, u32[]{:S(2)}, u32[]{:S(2)}) collective-permute-start(f32[8,1,8,128]{3,2,1,0:T(8,128)S(1)} %get-tuple-element.103), channel_id=1, source_target_pairs={{16,0},{32,16},{48,32},{64,48},{80,64},{96,80},{112,96},{128,112},... | collective-permute-start | bytes 98312 | tf_op jit(solution)/shard_map/ppermute | solution.py:24
  88.9 7.9 %collective-permute-start.6 = (f32[8,1,8,128]{3,2,1,0:T(8,128)S(1)}, f32[8,1,8,128]{3,2,1,0:T(8,128)S(1)}, u32[]{:S(2)}, u32[]{:S(2)}) collective-permute-start(f32[8,1,8,128]{3,2,1,0:T(8,128)S(1)} %get-tuple-element.104), channel_id=1, source_target_pairs={{0,16},{16,32},{32,48},{48,64},{64,80},{80,96},{96,112},{112,128},... | collective-permute-start | bytes 98312 | tf_op jit(solution)/shard_map/ppermute | solution.py:21
  96.9 5.9 %collective-permute-start.9 = (f32[8,6,1,128]{3,2,1,0:T(1,128)S(1)}, f32[8,6,1,128]{3,2,1,0:T(1,128)S(1)}, u32[]{:S(2)}, u32[]{:S(2)}) collective-permute-start(f32[8,6,1,128]{3,2,1,0:T(1,128)S(1)} %get-tuple-element.89), channel_id=1, source_target_pairs={{4,0},{8,4},{12,8},{0,12},{5,1},{9,5},{13,9},{1,13},{6,2},{10,6},{... | collective-permute-start | bytes 73736 | tf_op jit(solution)/shard_map/ppermute | solution.py:24
  98.8 6.9 %collective-permute-start.8 = (f32[8,6,1,128]{3,2,1,0:T(1,128)S(1)}, f32[8,6,1,128]{3,2,1,0:T(1,128)S(1)}, u32[]{:S(2)}, u32[]{:S(2)}) collective-permute-start(f32[8,6,1,128]{3,2,1,0:T(1,128)S(1)} %get-tuple-element.90), channel_id=1, source_target_pairs={{0,4},{4,8},{8,12},{12,0},{1,5},{5,9},{9,13},{13,1},{2,6},{6,10},{... | collective-permute-start | bytes 73736 | tf_op jit(solution)/shard_map/ppermute | solution.py:21
  106.0 7.2 %collective-permute-start.10 = (f32[8,6,10,1]{3,2,1,0:T(8,128)S(1)}, f32[8,6,10,1]{3,2,1,0:T(8,128)S(1)}, u32[]{:S(2)}, u32[]{:S(2)}) collective-permute-start(f32[8,6,10,1]{3,2,1,0:T(8,128)S(1)} %get-tuple-element.69), channel_id=1, source_target_pairs={{1,0},{2,1},{3,2},{0,3},{5,4},{6,5},{7,6},{4,7},{9,8},{10,9},{11,1... | collective-permute-start | bytes 5768 | tf_op jit(solution)/shard_map/ppermute | solution.py:24
  107.9 12.8 %collective-permute-start.11 = (f32[8,6,10,1]{3,2,1,0:T(8,128)S(1)}, f32[8,6,10,1]{3,2,1,0:T(8,128)S(1)}, u32[]{:S(2)}, u32[]{:S(2)}) collective-permute-start(f32[8,6,10,1]{3,2,1,0:T(8,128)S(1)} %get-tuple-element.70), channel_id=1, source_target_pairs={{0,1},{1,2},{2,3},{3,0},{4,5},{5,6},{6,7},{7,4},{8,9},{9,10},{10,1... | collective-permute-start | bytes 5768 | tf_op jit(solution)/shard_map/ppermute | solution.py:21
  123.7 5.9 %collective-permute-start.13 = (f32[8,1,8,128]{3,2,1,0:T(8,128)S(1)}, f32[8,1,8,128]{3,2,1,0:T(8,128)S(1)}, u32[]{:S(2)}, u32[]{:S(2)}) collective-permute-start(f32[8,1,8,128]{3,2,1,0:T(8,128)S(1)} %get-tuple-element.99), channel_id=1, source_target_pairs={{16,0},{32,16},{48,32},{64,48},{80,64},{96,80},{112,96},{128,112},... | collective-permute-start | bytes 98312 | tf_op jit(solution)/shard_map/ppermute | solution.py:24
  125.9 7.9 %collective-permute-start.12 = (f32[8,1,8,128]{3,2,1,0:T(8,128)S(1)}, f32[8,1,8,128]{3,2,1,0:T(8,128)S(1)}, u32[]{:S(2)}, u32[]{:S(2)}) collective-permute-start(f32[8,1,8,128]{3,2,1,0:T(8,128)S(1)} %get-tuple-element.100), channel_id=1, source_target_pairs={{0,16},{16,32},{32,48},{48,64},{64,80},{80,96},{96,112},{112,128},... | collective-permute-start | bytes 98312 | tf_op jit(solution)/shard_map/ppermute | solution.py:21
  133.9 5.9 %collective-permute-start.15 = (f32[8,6,1,128]{3,2,1,0:T(1,128)S(1)}, f32[8,6,1,128]{3,2,1,0:T(1,128)S(1)}, u32[]{:S(2)}, u32[]{:S(2)}) collective-permute-start(f32[8,6,1,128]{3,2,1,0:T(1,128)S(1)} %get-tuple-element.87), channel_id=1, source_target_pairs={{4,0},{8,4},{12,8},{0,12},{5,1},{9,5},{13,9},{1,13},{6,2},{10,6},{... | collective-permute-start | bytes 73736 | tf_op jit(solution)/shard_map/ppermute | solution.py:24
  135.8 6.9 %collective-permute-start.14 = (f32[8,6,1,128]{3,2,1,0:T(1,128)S(1)}, f32[8,6,1,128]{3,2,1,0:T(1,128)S(1)}, u32[]{:S(2)}, u32[]{:S(2)}) collective-permute-start(f32[8,6,1,128]{3,2,1,0:T(1,128)S(1)} %get-tuple-element.88), channel_id=1, source_target_pairs={{0,4},{4,8},{8,12},{12,0},{1,5},{5,9},{9,13},{13,1},{2,6},{6,10},{... | collective-permute-start | bytes 73736 | tf_op jit(solution)/shard_map/ppermute | solution.py:21
  143.0 9.6 %collective-permute-start.16 = (f32[8,6,10,1]{3,2,1,0:T(8,128)S(1)}, f32[8,6,10,1]{3,2,1,0:T(8,128)S(1)}, u32[]{:S(2)}, u32[]{:S(2)}) collective-permute-start(f32[8,6,10,1]{3,2,1,0:T(8,128)S(1)} %get-tuple-element.67), channel_id=1, source_target_pairs={{1,0},{2,1},{3,2},{0,3},{5,4},{6,5},{7,6},{4,7},{9,8},{10,9},{11,1... | collective-permute-start | bytes 5768 | tf_op jit(solution)/shard_map/ppermute | solution.py:24
  144.9 10.6 %collective-permute-start.17 = (f32[8,6,10,1]{3,2,1,0:T(8,128)S(1)}, f32[8,6,10,1]{3,2,1,0:T(8,128)S(1)}, u32[]{:S(2)}, u32[]{:S(2)}) collective-permute-start(f32[8,6,10,1]{3,2,1,0:T(8,128)S(1)} %get-tuple-element.68), channel_id=1, source_target_pairs={{0,1},{1,2},{2,3},{3,0},{4,5},{5,6},{6,7},{7,4},{8,9},{9,10},{10,1... | collective-permute-start | bytes 5768 | tf_op jit(solution)/shard_map/ppermute | solution.py:21
  158.2 5.9 %collective-permute-start.19 = (f32[8,1,8,128]{3,2,1,0:T(8,128)S(1)}, f32[8,1,8,128]{3,2,1,0:T(8,128)S(1)}, u32[]{:S(2)}, u32[]{:S(2)}) collective-permute-start(f32[8,1,8,128]{3,2,1,0:T(8,128)S(1)} %get-tuple-element.95), channel_id=1, source_target_pairs={{16,0},{32,16},{48,32},{64,48},{80,64},{96,80},{112,96},{128,112},... | collective-permute-start | bytes 98312 | tf_op jit(solution)/shard_map/ppermute | solution.py:24
  160.1 7.9 %collective-permute-start.18 = (f32[8,1,8,128]{3,2,1,0:T(8,128)S(1)}, f32[8,1,8,128]{3,2,1,0:T(8,128)S(1)}, u32[]{:S(2)}, u32[]{:S(2)}) collective-permute-start(f32[8,1,8,128]{3,2,1,0:T(8,128)S(1)} %get-tuple-element.96), channel_id=1, source_target_pairs={{0,16},{16,32},{32,48},{48,64},{64,80},{80,96},{96,112},{112,128},... | collective-permute-start | bytes 98312 | tf_op jit(solution)/shard_map/ppermute | solution.py:21
  168.1 5.9 %collective-permute-start.21 = (f32[8,6,1,128]{3,2,1,0:T(1,128)S(1)}, f32[8,6,1,128]{3,2,1,0:T(1,128)S(1)}, u32[]{:S(2)}, u32[]{:S(2)}) collective-permute-start(f32[8,6,1,128]{3,2,1,0:T(1,128)S(1)} %get-tuple-element.85), channel_id=1, source_target_pairs={{4,0},{8,4},{12,8},{0,12},{5,1},{9,5},{13,9},{1,13},{6,2},{10,6},{... | collective-permute-start | bytes 73736 | tf_op jit(solution)/shard_map/ppermute | solution.py:24
  170.2 6.9 %collective-permute-start.20 = (f32[8,6,1,128]{3,2,1,0:T(1,128)S(1)}, f32[8,6,1,128]{3,2,1,0:T(1,128)S(1)}, u32[]{:S(2)}, u32[]{:S(2)}) collective-permute-start(f32[8,6,1,128]{3,2,1,0:T(1,128)S(1)} %get-tuple-element.86), channel_id=1, source_target_pairs={{0,4},{4,8},{8,12},{12,0},{1,5},{5,9},{9,13},{13,1},{2,6},{6,10},{... | collective-permute-start | bytes 73736 | tf_op jit(solution)/shard_map/ppermute | solution.py:21
  177.4 7.2 %collective-permute-start.22 = (f32[8,6,10,1]{3,2,1,0:T(8,128)S(1)}, f32[8,6,10,1]{3,2,1,0:T(8,128)S(1)}, u32[]{:S(2)}, u32[]{:S(2)}) collective-permute-start(f32[8,6,10,1]{3,2,1,0:T(8,128)S(1)} %get-tuple-element.65), channel_id=1, source_target_pairs={{1,0},{2,1},{3,2},{0,3},{5,4},{6,5},{7,6},{4,7},{9,8},{10,9},{11,1... | collective-permute-start | bytes 5768 | tf_op jit(solution)/shard_map/ppermute | solution.py:24
  179.3 12.8 %collective-permute-start.23 = (f32[8,6,10,1]{3,2,1,0:T(8,128)S(1)}, f32[8,6,10,1]{3,2,1,0:T(8,128)S(1)}, u32[]{:S(2)}, u32[]{:S(2)}) collective-permute-start(f32[8,6,10,1]{3,2,1,0:T(8,128)S(1)} %get-tuple-element.66), channel_id=1, source_target_pairs={{0,1},{1,2},{2,3},{3,0},{4,5},{5,6},{6,7},{7,4},{8,9},{9,10},{10,1... | collective-permute-start | bytes 5768 | tf_op jit(solution)/shard_map/ppermute | solution.py:21
  194.4 8.0 %collective-permute-start.24 = (f32[2,1,8,128]{3,2,1,0:T(8,128)}, f32[2,1,8,128]{3,2,1,0:T(8,128)S(1)}, u32[]{:S(2)}, u32[]{:S(2)}) collective-permute-start(f32[2,1,8,128]{3,2,1,0:T(8,128)} %get-tuple-element.139), channel_id=1, source_target_pairs={{0,16},{16,32},{32,48},{48,64},{64,80},{80,96},{96,112},{112,128},... | collective-permute-start | bytes 24584 | tf_op jit(solution)/shard_map/ppermute | solution.py:21
  196.3 7.6 %collective-permute-start.25 = (f32[2,1,8,128]{3,2,1,0:T(8,128)}, f32[2,1,8,128]{3,2,1,0:T(8,128)}, u32[]{:S(2)}, u32[]{:S(2)}) collective-permute-start(f32[2,1,8,128]{3,2,1,0:T(8,128)} %get-tuple-element.140), channel_id=1, source_target_pairs={{16,0},{32,16},{48,32},{64,48},{80,64},{96,80},{112,96},{128,112},... | collective-permute-start | bytes 24584 | tf_op jit(solution)/shard_map/ppermute | solution.py:24
  205.4 9.1 %collective-permute-start.26 = (f32[2,6,1,128]{3,2,1,0:T(1,128)}, f32[2,6,1,128]{3,2,1,0:T(1,128)}, u32[]{:S(2)}, u32[]{:S(2)}) collective-permute-start(f32[2,6,1,128]{3,2,1,0:T(1,128)} %get-tuple-element.131), channel_id=1, source_target_pairs={{0,4},{4,8},{8,12},{12,0},{1,5},{5,9},{9,13},{13,1},{2,6},{6,10},{... | collective-permute-start | bytes 18440 | tf_op jit(solution)/shard_map/ppermute | solution.py:21
  207.9 6.6 %collective-permute-start.27 = (f32[2,6,1,128]{3,2,1,0:T(1,128)}, f32[2,6,1,128]{3,2,1,0:T(1,128)}, u32[]{:S(2)}, u32[]{:S(2)}) collective-permute-start(f32[2,6,1,128]{3,2,1,0:T(1,128)} %get-tuple-element.132), channel_id=1, source_target_pairs={{4,0},{8,4},{12,8},{0,12},{5,1},{9,5},{13,9},{1,13},{6,2},{10,6},{... | collective-permute-start | bytes 18440 | tf_op jit(solution)/shard_map/ppermute | solution.py:24
  215.4 8.3 %collective-permute-start.29 = (f32[2,6,10,1]{3,2,1,0:T(8,128)S(1)}, f32[2,6,10,1]{3,2,1,0:T(8,128)S(1)}, u32[]{:S(2)}, u32[]{:S(2)}) collective-permute-start(f32[2,6,10,1]{3,2,1,0:T(8,128)S(1)} %get-tuple-element.115), channel_id=1, source_target_pairs={{0,1},{1,2},{2,3},{3,0},{4,5},{5,6},{6,7},{7,4},{8,9},{9,10},{10,1... | collective-permute-start | bytes 1448 | tf_op jit(solution)/shard_map/ppermute | solution.py:21
  217.3 7.3 %collective-permute-start.28 = (f32[2,6,10,1]{3,2,1,0:T(8,128)S(1)}, f32[2,6,10,1]{3,2,1,0:T(8,128)S(1)}, u32[]{:S(2)}, u32[]{:S(2)}) collective-permute-start(f32[2,6,10,1]{3,2,1,0:T(8,128)S(1)} %get-tuple-element.116), channel_id=1, source_target_pairs={{1,0},{2,1},{3,2},{0,3},{5,4},{6,5},{7,6},{4,7},{9,8},{10,9},{11,1... | collective-permute-start | bytes 1448 | tf_op jit(solution)/shard_map/ppermute | solution.py:24
  235.2 8.8 %collective-permute-start.30 = (f32[2,1,8,128]{3,2,1,0:T(8,128)S(1)}, f32[2,1,8,128]{3,2,1,0:T(8,128)S(1)}, u32[]{:S(2)}, u32[]{:S(2)}) collective-permute-start(f32[2,1,8,128]{3,2,1,0:T(8,128)S(1)} %get-tuple-element.137), channel_id=1, source_target_pairs={{0,16},{16,32},{32,48},{48,64},{64,80},{80,96},{96,112},{112,128},... | collective-permute-start | bytes 24584 | tf_op jit(solution)/shard_map/ppermute | solution.py:21
  237.2 7.9 %collective-permute-start.31 = (f32[2,1,8,128]{3,2,1,0:T(8,128)S(1)}, f32[2,1,8,128]{3,2,1,0:T(8,128)S(1)}, u32[]{:S(2)}, u32[]{:S(2)}) collective-permute-start(f32[2,1,8,128]{3,2,1,0:T(8,128)S(1)} %get-tuple-element.138), channel_id=1, source_target_pairs={{16,0},{32,16},{48,32},{64,48},{80,64},{96,80},{112,96},{128,112},... | collective-permute-start | bytes 24584 | tf_op jit(solution)/shard_map/ppermute | solution.py:24
  245.1 8.0 %collective-permute-start.32 = (f32[2,6,1,128]{3,2,1,0:T(1,128)S(1)}, f32[2,6,1,128]{3,2,1,0:T(1,128)S(1)}, u32[]{:S(2)}, u32[]{:S(2)}) collective-permute-start(f32[2,6,1,128]{3,2,1,0:T(1,128)S(1)} %get-tuple-element.127), channel_id=1, source_target_pairs={{0,4},{4,8},{8,12},{12,0},{1,5},{5,9},{9,13},{13,1},{2,6},{6,10},{... | collective-permute-start | bytes 18440 | tf_op jit(solution)/shard_map/ppermute | solution.py:21
  247.0 6.4 %collective-permute-start.33 = (f32[2,6,1,128]{3,2,1,0:T(1,128)S(1)}, f32[2,6,1,128]{3,2,1,0:T(1,128)S(1)}, u32[]{:S(2)}, u32[]{:S(2)}) collective-permute-start(f32[2,6,1,128]{3,2,1,0:T(1,128)S(1)} %get-tuple-element.128), channel_id=1, source_target_pairs={{4,0},{8,4},{12,8},{0,12},{5,1},{9,5},{13,9},{1,13},{6,2},{10,6},{... | collective-permute-start | bytes 18440 | tf_op jit(solution)/shard_map/ppermute | solution.py:24
  253.6 7.4 %collective-permute-start.35 = (f32[2,6,10,1]{3,2,1,0:T(8,128)S(1)}, f32[2,6,10,1]{3,2,1,0:T(8,128)S(1)}, u32[]{:S(2)}, u32[]{:S(2)}) collective-permute-start(f32[2,6,10,1]{3,2,1,0:T(8,128)S(1)} %get-tuple-element.113), channel_id=1, source_target_pairs={{0,1},{1,2},{2,3},{3,0},{4,5},{5,6},{6,7},{7,4},{8,9},{9,10},{10,1... | collective-permute-start | bytes 1448 | tf_op jit(solution)/shard_map/ppermute | solution.py:21
  255.5 7.3 %collective-permute-start.34 = (f32[2,6,10,1]{3,2,1,0:T(8,128)S(1)}, f32[2,6,10,1]{3,2,1,0:T(8,128)S(1)}, u32[]{:S(2)}, u32[]{:S(2)}) collective-permute-start(f32[2,6,10,1]{3,2,1,0:T(8,128)S(1)} %get-tuple-element.114), channel_id=1, source_target_pairs={{1,0},{2,1},{3,2},{0,3},{5,4},{6,5},{7,6},{4,7},{9,8},{10,9},{11,1... | collective-permute-start | bytes 1448 | tf_op jit(solution)/shard_map/ppermute | solution.py:24
  272.9 8.7 %collective-permute-start.36 = (f32[2,1,8,128]{3,2,1,0:T(8,128)S(1)}, f32[2,1,8,128]{3,2,1,0:T(8,128)S(1)}, u32[]{:S(2)}, u32[]{:S(2)}) collective-permute-start(f32[2,1,8,128]{3,2,1,0:T(8,128)S(1)} %get-tuple-element.135), channel_id=1, source_target_pairs={{0,16},{16,32},{32,48},{48,64},{64,80},{80,96},{96,112},{112,128},... | collective-permute-start | bytes 24584 | tf_op jit(solution)/shard_map/ppermute | solution.py:21
  274.9 7.8 %collective-permute-start.37 = (f32[2,1,8,128]{3,2,1,0:T(8,128)S(1)}, f32[2,1,8,128]{3,2,1,0:T(8,128)S(1)}, u32[]{:S(2)}, u32[]{:S(2)}) collective-permute-start(f32[2,1,8,128]{3,2,1,0:T(8,128)S(1)} %get-tuple-element.136), channel_id=1, source_target_pairs={{16,0},{32,16},{48,32},{64,48},{80,64},{96,80},{112,96},{128,112},... | collective-permute-start | bytes 24584 | tf_op jit(solution)/shard_map/ppermute | solution.py:24
  282.7 8.3 %collective-permute-start.38 = (f32[2,6,1,128]{3,2,1,0:T(1,128)S(1)}, f32[2,6,1,128]{3,2,1,0:T(1,128)S(1)}, u32[]{:S(2)}, u32[]{:S(2)}) collective-permute-start(f32[2,6,1,128]{3,2,1,0:T(1,128)S(1)} %get-tuple-element.123), channel_id=1, source_target_pairs={{0,4},{4,8},{8,12},{12,0},{1,5},{5,9},{9,13},{13,1},{2,6},{6,10},{... | collective-permute-start | bytes 18440 | tf_op jit(solution)/shard_map/ppermute | solution.py:21
  286.1 5.5 %collective-permute-start.39 = (f32[2,6,1,128]{3,2,1,0:T(1,128)S(1)}, f32[2,6,1,128]{3,2,1,0:T(1,128)S(1)}, u32[]{:S(2)}, u32[]{:S(2)}) collective-permute-start(f32[2,6,1,128]{3,2,1,0:T(1,128)S(1)} %get-tuple-element.124), channel_id=1, source_target_pairs={{4,0},{8,4},{12,8},{0,12},{5,1},{9,5},{13,9},{1,13},{6,2},{10,6},{... | collective-permute-start | bytes 18440 | tf_op jit(solution)/shard_map/ppermute | solution.py:24
  291.8 7.4 %collective-permute-start.41 = (f32[2,6,10,1]{3,2,1,0:T(8,128)S(1)}, f32[2,6,10,1]{3,2,1,0:T(8,128)S(1)}, u32[]{:S(2)}, u32[]{:S(2)}) collective-permute-start(f32[2,6,10,1]{3,2,1,0:T(8,128)S(1)} %get-tuple-element.111), channel_id=1, source_target_pairs={{0,1},{1,2},{2,3},{3,0},{4,5},{5,6},{6,7},{7,4},{8,9},{9,10},{10,1... | collective-permute-start | bytes 1448 | tf_op jit(solution)/shard_map/ppermute | solution.py:21
  293.7 7.3 %collective-permute-start.40 = (f32[2,6,10,1]{3,2,1,0:T(8,128)S(1)}, f32[2,6,10,1]{3,2,1,0:T(8,128)S(1)}, u32[]{:S(2)}, u32[]{:S(2)}) collective-permute-start(f32[2,6,10,1]{3,2,1,0:T(8,128)S(1)} %get-tuple-element.112), channel_id=1, source_target_pairs={{1,0},{2,1},{3,2},{0,3},{5,4},{6,5},{7,6},{4,7},{9,8},{10,9},{11,1... | collective-permute-start | bytes 1448 | tf_op jit(solution)/shard_map/ppermute | solution.py:24
  308.5 8.7 %collective-permute-start.42 = (f32[2,1,8,128]{3,2,1,0:T(8,128)S(1)}, f32[2,1,8,128]{3,2,1,0:T(8,128)S(1)}, u32[]{:S(2)}, u32[]{:S(2)}) collective-permute-start(f32[2,1,8,128]{3,2,1,0:T(8,128)S(1)} %get-tuple-element.133), channel_id=1, source_target_pairs={{0,16},{16,32},{32,48},{48,64},{64,80},{80,96},{96,112},{112,128},... | collective-permute-start | bytes 24584 | tf_op jit(solution)/shard_map/ppermute | solution.py:21
  310.4 7.8 %collective-permute-start.43 = (f32[2,1,8,128]{3,2,1,0:T(8,128)S(1)}, f32[2,1,8,128]{3,2,1,0:T(8,128)S(1)}, u32[]{:S(2)}, u32[]{:S(2)}) collective-permute-start(f32[2,1,8,128]{3,2,1,0:T(8,128)S(1)} %get-tuple-element.134), channel_id=1, source_target_pairs={{16,0},{32,16},{48,32},{64,48},{80,64},{96,80},{112,96},{128,112},... | collective-permute-start | bytes 24584 | tf_op jit(solution)/shard_map/ppermute | solution.py:24
  318.2 8.0 %collective-permute-start.44 = (f32[2,6,1,128]{3,2,1,0:T(1,128)S(1)}, f32[2,6,1,128]{3,2,1,0:T(1,128)S(1)}, u32[]{:S(2)}, u32[]{:S(2)}) collective-permute-start(f32[2,6,1,128]{3,2,1,0:T(1,128)S(1)} %get-tuple-element.119), channel_id=1, source_target_pairs={{0,4},{4,8},{8,12},{12,0},{1,5},{5,9},{9,13},{13,1},{2,6},{6,10},{... | collective-permute-start | bytes 18440 | tf_op jit(solution)/shard_map/ppermute | solution.py:21
  322.1 5.5 %collective-permute-start.45 = (f32[2,6,1,128]{3,2,1,0:T(1,128)S(1)}, f32[2,6,1,128]{3,2,1,0:T(1,128)S(1)}, u32[]{:S(2)}, u32[]{:S(2)}) collective-permute-start(f32[2,6,1,128]{3,2,1,0:T(1,128)S(1)} %get-tuple-element.120), channel_id=1, source_target_pairs={{4,0},{8,4},{12,8},{0,12},{5,1},{9,5},{13,9},{1,13},{6,2},{10,6},{... | collective-permute-start | bytes 18440 | tf_op jit(solution)/shard_map/ppermute | solution.py:24
  327.8 7.4 %collective-permute-start.47 = (f32[2,6,10,1]{3,2,1,0:T(8,128)S(1)}, f32[2,6,10,1]{3,2,1,0:T(8,128)S(1)}, u32[]{:S(2)}, u32[]{:S(2)}) collective-permute-start(f32[2,6,10,1]{3,2,1,0:T(8,128)S(1)} %get-tuple-element.109), channel_id=1, source_target_pairs={{0,1},{1,2},{2,3},{3,0},{4,5},{5,6},{6,7},{7,4},{8,9},{9,10},{10,1... | collective-permute-start | bytes 1448 | tf_op jit(solution)/shard_map/ppermute | solution.py:21
  329.7 7.3 %collective-permute-start.46 = (f32[2,6,10,1]{3,2,1,0:T(8,128)S(1)}, f32[2,6,10,1]{3,2,1,0:T(8,128)S(1)}, u32[]{:S(2)}, u32[]{:S(2)}) collective-permute-start(f32[2,6,10,1]{3,2,1,0:T(8,128)S(1)} %get-tuple-element.110), channel_id=1, source_target_pairs={{1,0},{2,1},{3,2},{0,3},{5,4},{6,5},{7,6},{4,7},{9,8},{10,9},{11,1... | collective-permute-start | bytes 1448 | tf_op jit(solution)/shard_map/ppermute | solution.py:24
  (111 other events, 1595.5 us)
